TPU v7x, 256 devices: a whole 4x4x8 slice. The times are simulated.
256 devices in a mesh: seq: 32 (over z_hi, x, core), head: 8 (over y, z_lo).
Axes of the slice: x: 4, y: 4, z: 8 (z_hi: 4, z_lo: 2; z = z_hi * 2 + z_lo), core: 2. Of those that a mesh axis runs over, the one named last changes fastest.
Arguments:
- tokens: bfloat16 [4096, 3072], P('seq', 'head'), may hold values from -5 to 5, as said below
- norm_gains: float32 [5, 3072], replicated, may hold values from 0.25 to 1.75
- window: int32 [24], P('head'), may hold values from 16 to 128, as said below
- self_query: bfloat16 [3072, 3072], P(None, 'head')
- self_key_value: bfloat16 [2, 3072, 1024], P(None, None, 'head')
- self_output: bfloat16 [3072, 3072], P('head'), may hold values from -0.4375 to 0.4375
- shared_key_value: bfloat16 [2, 3072, 1024], P(None, None, 'head')
- cross_query: bfloat16 [3, 3072, 3072], P(None, 'seq', 'head')
- cross_output: bfloat16 [3, 3072, 3072], P(None, 'head', 'seq'), may hold values from -0.4375 to 0.4375
- key_blocks: int32 [3, 32, 16], P(None, 'seq'), may hold values from -1 to 31, as said below
Outputs:
- mixed: float32 [4096, 3072], P('seq', 'head')
Inputs may be any that keep to these rules, and one draw needn't show every extreme that they name: `tokens`: rows may hold near twins of the rows beside them. Some head has a window of exactly 128 and some head one of exactly 16. `key_blocks`: the row of query block b lists distinct blocks at or before b, the first being b itself; it holds min(16, b + 1) blocks and -1 in the remaining slots.
All inputs are finite; a program needn't handle non-finite values.
Results may differ from a plain program's by a relative error of at most 0.04.
Values may be sent and summed in bfloat16 or wider, within the bound.
A program may use at most 64 MiB of HBM per device.

v0:
```python
import jax
import jax.numpy as jnp
from jax import lax
from jax.sharding import PartitionSpec as P

HEAD_WIDTH = 128
KEY_BLOCK_TOKENS = 128
LISTED_BLOCKS = 16
SECTIONS = 3


EPSILON = 1e-06
MASKED = -1e30


def passed_along(value, axis, steps):
    count = lax.axis_size(axis)
    initial, last = (max(0, -steps), min(count, count - steps))
    return lax.ppermute(value, axis, [(source, source + steps) for source in range(initial, last)])


def softmax_rows(scores, allowed):
    scores = jnp.where(allowed, scores, MASKED)
    largest = jnp.max(scores, axis=-1, keepdims=True)
    weights = jnp.exp(scores - largest)
    return (weights / jnp.sum(weights, axis=-1, keepdims=True)).astype(jnp.bfloat16)


def body(
    tokens,
    norm_gains,
    window,
    self_query,
    self_key_value,
    self_output,
    shared_key_value,
    cross_query,
    cross_output,
    key_blocks,
):
    seq_rank = lax.axis_index("seq")
    row_count, local_width = tokens.shape
    kv_columns = self_key_value.shape[2]
    query_columns = self_query.shape[1]
    kv_heads = kv_columns // HEAD_WIDTH
    query_group_width = query_columns // kv_columns
    scale_factor = HEAD_WIDTH ** (-0.5)

    def normed_full(stream, gain_row):
        gathered = lax.all_gather(
            stream.astype(jnp.float32).astype(jnp.bfloat16), "head", axis=1, tiled=True
        ).astype(jnp.float32)
        factor = lax.rsqrt(jnp.mean(gathered * gathered, axis=1, keepdims=True) + EPSILON)
        return (gathered * factor * gain_row[None, :]).astype(jnp.bfloat16)

    def add_branch(stream, partial_value):
        summed = lax.psum_scatter(
            partial_value.astype(jnp.bfloat16), "head", scatter_dimension=1, tiled=True
        ).astype(jnp.float32)
        return stream.astype(jnp.float32) + summed

    def project(inputs, weight):
        return jnp.dot(inputs, weight, preferred_element_type=jnp.float32).astype(jnp.bfloat16)

    first = normed_full(tokens, norm_gains[0])
    query_matrix = project(first, self_query)
    keys_own = project(first, self_key_value[0])
    values_own = project(first, self_key_value[1])
    keys_prev, values_prev = passed_along((keys_own, values_own), "seq", 1)
    near_keys = jnp.concatenate([keys_prev, keys_own], axis=0).reshape(
        2 * row_count, kv_heads, HEAD_WIDTH
    )
    near_values = jnp.concatenate([values_prev, values_own], axis=0).reshape(
        2 * row_count, kv_heads, HEAD_WIDTH
    )
    query_heads = query_matrix.reshape(row_count, kv_heads, query_group_width, HEAD_WIDTH)
    scores = (
        jnp.einsum("tkgd,skd->kgts", query_heads, near_keys, preferred_element_type=jnp.float32)
        * scale_factor
    )
    offsets = (
        jnp.arange(row_count, dtype=jnp.int32)[:, None]
        + row_count
        - jnp.arange(2 * row_count, dtype=jnp.int32)[None, :]
    )
    key_pos = seq_rank * row_count - row_count + jnp.arange(2 * row_count, dtype=jnp.int32)
    window_bounds = window.reshape(kv_heads, query_group_width)
    allowed = (
        (offsets >= 0)[None, None]
        & (offsets[None, None] < window_bounds[:, :, None, None])
        & (key_pos >= 0)[None, None, None, :]
    )
    probs = softmax_rows(scores, allowed)
    context = jnp.einsum("kgts,skd->tkgd", probs, near_values, preferred_element_type=jnp.float32)
    context = context.astype(jnp.bfloat16).reshape(row_count, query_columns)
    stream = add_branch(tokens, jnp.dot(context, self_output, preferred_element_type=jnp.float32))
    cache_in = normed_full(stream, norm_gains[1])
    cached_key_rows = project(cache_in, shared_key_value[0])
    cached_value_rows = project(cache_in, shared_key_value[1])
    all_keys, all_values = (
        lax.all_gather(cached_key_rows, "seq", axis=0, tiled=True),
        lax.all_gather(cached_value_rows, "seq", axis=0, tiled=True),
    )
    key_lookup_matrix = all_keys.reshape(-1, KEY_BLOCK_TOKENS, kv_columns)
    value_lookup_matrix = all_values.reshape(-1, KEY_BLOCK_TOKENS, kv_columns)
    query_blocks = row_count // KEY_BLOCK_TOKENS
    inner = jnp.arange(KEY_BLOCK_TOKENS, dtype=jnp.int32)
    block_ids = seq_rank * query_blocks + jnp.arange(query_blocks, dtype=jnp.int32)
    query_pos = block_ids[:, None] * KEY_BLOCK_TOKENS + inner[None, :]
    for section in range(SECTIONS):
        section_in = normed_full(stream, norm_gains[2 + section])
        query_matrix = jnp.dot(
            section_in,
            lax.all_gather(cross_query[section], "seq", axis=0, tiled=True),
            preferred_element_type=jnp.float32,
        ).astype(jnp.bfloat16)
        lists = key_blocks[section]
        clamped_index = jnp.maximum(lists, 0)
        picked_keys = jnp.take(key_lookup_matrix, clamped_index.reshape(-1), axis=0).reshape(
            query_blocks, LISTED_BLOCKS * KEY_BLOCK_TOKENS, kv_heads, HEAD_WIDTH
        )
        picked_values = jnp.take(value_lookup_matrix, clamped_index.reshape(-1), axis=0).reshape(
            query_blocks, LISTED_BLOCKS * KEY_BLOCK_TOKENS, kv_heads, HEAD_WIDTH
        )
        query_heads = query_matrix.reshape(
            query_blocks, KEY_BLOCK_TOKENS, kv_heads, query_group_width, HEAD_WIDTH
        )
        scores = (
            jnp.einsum(
                "btkgd,bskd->bkgts", query_heads, picked_keys, preferred_element_type=jnp.float32
            )
            * scale_factor
        )
        listed_pos = (clamped_index[:, :, None] * KEY_BLOCK_TOKENS + inner[None, None, :]).reshape(
            query_blocks, LISTED_BLOCKS * KEY_BLOCK_TOKENS
        )
        present = jnp.repeat(lists >= 0, KEY_BLOCK_TOKENS, axis=1)
        allowed = present[:, None, :] & (listed_pos[:, None, :] <= query_pos[:, :, None])
        probs = softmax_rows(scores, allowed[:, None, None])
        context = jnp.einsum(
            "bkgts,bskd->btkgd", probs, picked_values, preferred_element_type=jnp.float32
        )
        context = context.astype(jnp.bfloat16).reshape(row_count, query_columns)
        partial_value = jnp.dot(
            context,
            lax.all_gather(cross_output[section], "seq", axis=1, tiled=True),
            preferred_element_type=jnp.float32,
        )
        stream = add_branch(stream, partial_value)
    return stream


def solution(mesh):
    placed = (
        P("seq", "head"),
        P(),
        P("head"),
        P(None, "head"),
        P(None, None, "head"),
        P("head", None),
        P(None, None, "head"),
        P(None, "seq", "head"),
        P(None, "head", "seq"),
        P(None, "seq", None),
    )
    return jax.shard_map(
        body, mesh=mesh, in_specs=placed, out_specs=P("seq", "head"), check_vma=False
    )
```

profile of v0, /device:TPU:4, one launch (start us, length us, event | category | flops | bytes accessed | tf_op | source)
XLA Modules:
  0.0 703.6 jit_solution(482095804169605450)
XLA Ops:
  8.4 32.0 %all_gather.37 = bf16[128,3072]{1,0:T(8,128)(2,1)S(1)} all-gather(bf16[128,384]{1,0:T(8,128)(2,1)} %param.12), channel_id=1, replica_groups=mesh['seq'=32,'head'=8] {'head'}, dimensions={1}, use_global_device_ids=true | all-gather | bytes 884736 | tf_op jit(solution)/shard_map/all_gather | solution.py:50
  44.8 3.2 collective-permute-start
  52.2 46.3 %reduce-scatter.13.cloned.1.call-done = bf16[384,128]{1,0:T(8,128)(2,1)} async-done(((bf16[3072,128]{1,0:T(8,128)(2,1)}), bf16[384,128]{1,0:T(8,128)(2,1)}) %reduce-scatter.13.cloned.1.call-update) | async-done | bytes 98320
  99.5 31.2 %all_gather.38 = bf16[128,3072]{1,0:T(8,128)(2,1)S(1)} all-gather(bf16[128,384]{1,0:T(8,128)(2,1)S(1)} %fusion.73), channel_id=1, replica_groups=mesh['seq'=32,'head'=8] {'head'}, dimensions={1}, use_global_device_ids=true | all-gather | bytes 884736 | tf_op jit(solution)/shard_map/all_gather | solution.py:50
  130.9 2.2 convolution_convert_fusion.7
  139.4 4.1 compare_and_fusion
  143.5 39.0 %all-gather.15.cloned.1.call-done = bf16[4096,128]{1,0:T(8,128)(2,1)} async-done(((bf16[128,128]{1,0:T(8,128)(2,1)}), bf16[4096,128]{1,0:T(8,128)(2,1)}) %all-gather.15.cloned.1.call-update) | async-done | bytes 1048592 | tf_op jit(solution)/shard_map/all_gather | solution.py:102
  182.5 2.7 gather_fusion
  185.2 49.4 %all-gather.17.cloned.1.call-done = bf16[4096,128]{1,0:T(8,128)(2,1)} async-done(((bf16[128,128]{1,0:T(8,128)(2,1)}), bf16[4096,128]{1,0:T(8,128)(2,1)}) %all-gather.17.cloned.1.call-update) | async-done | bytes 1048592 | tf_op jit(solution)/shard_map/all_gather | solution.py:101
  234.6 2.7 gather_fusion.1
  237.3 2.4 broadcast_select_fusion.4
  239.7 49.5 %all-gather.19.cloned.1.call-done = bf16[1,3072,384]{2,1,0:T(8,128)(2,1)} async-done(((bf16[1,96,384]{2,1,0:T(8,128)(2,1)}), bf16[1,3072,384]{2,1,0:T(8,128)(2,1)}) %all-gather.19.cloned.1.call-update) | async-done | bytes 2359312 | tf_op jit(solution)/shard_map/all_gather | solution.py:114
  289.2 2.3 fusion.43
  295.2 48.1 %all-gather.21.cloned.1.call-done = bf16[1,384,3072]{1,2,0:T(8,128)(2,1)} async-done(((bf16[1,384,96]{1,2,0:T(8,128)(2,1)}), bf16[1,384,3072]{1,2,0:T(8,128)(2,1)}) %all-gather.21.cloned.1.call-update) | async-done | bytes 2359312 | tf_op jit(solution)/shard_map/all_gather | solution.py:146
  343.3 2.6 convolution_convert_fusion.2
  350.6 2.7 gather_fusion.5
  353.3 2.7 gather_fusion.2
  355.9 2.7 gather_fusion.3
  358.6 3.0 broadcast_select_fusion
  361.6 26.7 %reduce-scatter.15.cloned.1.call-done = bf16[384,128]{1,0:T(8,128)(2,1)} async-done(((bf16[3072,128]{1,0:T(8,128)(2,1)}), bf16[384,128]{1,0:T(8,128)(2,1)}) %reduce-scatter.15.cloned.1.call-update) | async-done | bytes 98320
  389.4 31.4 %all_gather.43 = bf16[128,3072]{1,0:T(8,128)(2,1)S(1)} all-gather(bf16[128,384]{1,0:T(8,128)(2,1)S(1)} %fusion.79), channel_id=1, replica_groups=mesh['seq'=32,'head'=8] {'head'}, dimensions={1}, use_global_device_ids=true | all-gather | bytes 884736 | tf_op jit(solution)/shard_map/all_gather | solution.py:50
  421.0 21.5 %all-gather.23.cloned.1.call-done = bf16[1,3072,384]{2,1,0:T(8,128)(2,1)} async-done(((bf16[1,96,384]{2,1,0:T(8,128)(2,1)}), bf16[1,3072,384]{2,1,0:T(8,128)(2,1)}) %all-gather.23.cloned.1.call-update) | async-done | bytes 2359312 | tf_op jit(solution)/shard_map/all_gather | solution.py:114
  442.4 2.3 fusion.46
  448.5 48.3 %all-gather.25.cloned.1.call-done = bf16[1,384,3072]{1,2,0:T(8,128)(2,1)} async-done(((bf16[1,384,96]{1,2,0:T(8,128)(2,1)}), bf16[1,384,3072]{1,2,0:T(8,128)(2,1)}) %all-gather.25.cloned.1.call-update) | async-done | bytes 2359312 | tf_op jit(solution)/shard_map/all_gather | solution.py:146
  496.8 2.6 convolution_convert_fusion.1
  501.9 39.7 %reduce-scatter.17.cloned.1.call-done = bf16[384,128]{1,0:T(8,128)(2,1)} async-done(((bf16[3072,128]{1,0:T(8,128)(2,1)}), bf16[384,128]{1,0:T(8,128)(2,1)}) %reduce-scatter.17.cloned.1.call-update) | async-done | bytes 98320
  542.6 31.3 %all_gather.46 = bf16[128,3072]{1,0:T(8,128)(2,1)S(1)} all-gather(bf16[128,384]{1,0:T(8,128)(2,1)S(1)} %fusion.74), channel_id=1, replica_groups=mesh['seq'=32,'head'=8] {'head'}, dimensions={1}, use_global_device_ids=true | all-gather | bytes 884736 | tf_op jit(solution)/shard_map/all_gather | solution.py:50
  574.2 21.6 %all-gather.27.cloned.1.call-done = bf16[1,3072,384]{2,1,0:T(8,128)(2,1)} async-done(((bf16[1,96,384]{2,1,0:T(8,128)(2,1)}), bf16[1,3072,384]{2,1,0:T(8,128)(2,1)}) %all-gather.27.cloned.1.call-update) | async-done | bytes 2359312 | tf_op jit(solution)/shard_map/all_gather | solution.py:114
  595.7 2.9 fusion.49
  603.9 46.1 %all-gather.29.cloned.1.call-done = bf16[1,384,3072]{1,2,0:T(8,128)(2,1)} async-done(((bf16[1,384,96]{1,2,0:T(8,128)(2,1)}), bf16[1,384,3072]{1,2,0:T(8,128)(2,1)}) %all-gather.29.cloned.1.call-update) | async-done | bytes 2359312 | tf_op jit(solution)/shard_map/all_gather | solution.py:146
  650.1 2.6 convolution_convert_fusion
  653.9 41.1 %reduce-scatter.19.cloned.1.call-done = bf16[384,128]{1,0:T(8,128)(2,1)} async-done(((bf16[3072,128]{1,0:T(8,128)(2,1)}), bf16[384,128]{1,0:T(8,128)(2,1)}) %reduce-scatter.19.cloned.1.call-update) | async-done | bytes 98320
  (108 shorter events, 43.0 us)
Async XLA Ops:
  6.5 43.8 %copy-start = (bf16[384,3072]{1,0:T(8,128)(2,1)S(1)}, bf16[384,3072]{1,0:T(8,128)(2,1)}, u32[]{:S(2)}) copy-start(bf16[384,3072]{1,0:T(8,128)(2,1)} %param.17) | copy-start | bytes 7077892
  6.5 91.9 %reduce-scatter.13.cloned.1.call-start = ((), (), s32[]{:S(2)}) async-start(), calls=%async_computation.12 | async-start | bytes 884736
  6.5 37.8 %copy-start.7 = (bf16[2,3072,128]{2,1,0:T(8,128)(2,1)S(1)}, bf16[2,3072,128]{2,1,0:T(8,128)(2,1)}, u32[]{:S(2)}) copy-start(bf16[2,3072,128]{2,1,0:T(8,128)(2,1)} %param.16) | copy-start | bytes 4718596
  40.7 7.4 %copy-start.6 = (bf16[3072,384]{1,0:T(8,128)(2,1)S(1)}, bf16[3072,384]{1,0:T(8,128)(2,1)}, u32[]{:S(2)}) copy-start(bf16[3072,384]{1,0:T(8,128)(2,1)} %param.15) | copy-start | bytes 7077892
  42.5 6.5 collective-permute-start.1
  44.8 4.1 copy-start.8
  44.8 5.2 collective-permute-start
  50.3 49.1 %copy-start.1 = (bf16[128,384]{1,0:T(8,128)(2,1)S(1)}, bf16[128,384]{1,0:T(8,128)(2,1)}, u32[]{:S(2)}) copy-start(bf16[128,384]{1,0:T(8,128)(2,1)} %param.12) | copy-start | bytes 294916
  52.1 130.4 %all-gather.15.cloned.1.call-start = ((), (), s32[]{:S(2)}) async-start(), calls=%async_computation.4 | async-start | bytes 1081344 | tf_op jit(solution)/shard_map/all_gather | solution.py:102
  133.1 5.8 copy-start.5
  133.1 101.4 %all-gather.17.cloned.1.call-start = ((), (), s32[]{:S(2)}) async-start(), calls=%async_computation.5 | async-start | bytes 1081344 | tf_op jit(solution)/shard_map/all_gather | solution.py:101
  135.4 153.8 %all-gather.19.cloned.1.call-start = ((), (), s32[]{:S(2)}) async-start(), calls=%async_computation.6 | async-start | bytes 2433024 | tf_op jit(solution)/shard_map/all_gather | solution.py:114
  137.1 206.3 %all-gather.21.cloned.1.call-start = ((), (), s32[]{:S(2)}) async-start(), calls=%async_computation.7 | async-start | bytes 2433024 | tf_op jit(solution)/shard_map/all_gather | solution.py:146
  138.8 249.5 %reduce-scatter.15.cloned.1.call-start = ((), (), s32[]{:S(2)}) async-start(), calls=%async_computation.13 | async-start | bytes 884736
  293.4 1.0 copy-start.4
  347.1 95.3 %all-gather.23.cloned.1.call-start = ((), (), s32[]{:S(2)}) async-start(), calls=%async_computation.8 | async-start | bytes 2433024 | tf_op jit(solution)/shard_map/all_gather | solution.py:114
  347.9 148.9 %all-gather.25.cloned.1.call-start = ((), (), s32[]{:S(2)}) async-start(), calls=%async_computation.9 | async-start | bytes 2433024 | tf_op jit(solution)/shard_map/all_gather | solution.py:146
  348.6 192.9 %reduce-scatter.17.cloned.1.call-start = ((), (), s32[]{:S(2)}) async-start(), calls=%async_computation.14 | async-start | bytes 884736
  446.7 1.0 copy-start.3
  500.5 95.2 %all-gather.27.cloned.1.call-start = ((), (), s32[]{:S(2)}) async-start(), calls=%async_computation.10 | async-start | bytes 2433024 | tf_op jit(solution)/shard_map/all_gather | solution.py:114
  501.1 149.0 %all-gather.29.cloned.1.call-start = ((), (), s32[]{:S(2)}) async-start(), calls=%async_computation.11 | async-start | bytes 2433024 | tf_op jit(solution)/shard_map/all_gather | solution.py:146
  501.8 193.2 %reduce-scatter.19.cloned.1.call-start = ((), (), s32[]{:S(2)}) async-start(), calls=%async_computation.15 | async-start | bytes 884736
  601.5 1.0 copy-start.2
Sparse Core Ops, SparseCore 0:
  52.2 46.1 reduce-scatter.12
  133.2 49.1 all-gather.14
  185.0 49.4 all-gather.16
  237.0 52.1 all-gather.18
  291.6 51.7 all-gather.20
  347.3 40.9 reduce-scatter.14
  390.8 51.5 all-gather.22
  445.0 51.7 all-gather.24
  500.6 40.9 reduce-scatter.16
  544.0 51.7 all-gather.26
  598.3 51.7 all-gather.28
  654.0 40.9 reduce-scatter.18
where the time goes:
time: 705 us; the launch traced here: 704 us
  waiting for transfers between devices  481 us (68%)
  blocking collectives  126 us (18%)
  local copies, waits for them, and re-layouts  32.8 us (5%)
  matrix products  31.8 us (5%)
  between operations  14 us (2%)
  other arithmetic  12.8 us (2%)
    unnamed x16, waiting for transfers between devices  156 us
    all_gather x3, waiting for transfers between devices, body(): lax.all_gather(cross_output[section], 'seq', axis=1, tiled=True)  143 us
    all_gather x4, blocking collectives, normed_full(): lax.all_gather(stream.astype(jnp.float32).astype(jnp.bfloat16), 'head', a...  126 us
    all_gather x3, waiting for transfers between devices, body(): lax.all_gather(cross_query[section], 'seq', axis=0, tiled=True)  92.5 us
    all_gather x1, waiting for transfers between devices, body(): lax.all_gather(cached_key_rows, 'seq', axis=0, tiled=True)  49.4 us
    all_gather x1, waiting for transfers between devices, body(): lax.all_gather(cached_value_rows, 'seq', axis=0, tiled=True)  39 us
  transfers between devices with their start and end apart: 14, of which 13 were waited for; matrix products, arithmetic and copies ran while one was open for 8% of the time, Pallas kernels for 0%

commit v1 on v0

v1 whole, which is shorter than its diff:
```python
import math

import jax
import jax.numpy as jnp
from jax import lax
from jax.experimental import pallas as pl
from jax.experimental.pallas import tpu as pltpu
from jax.sharding import PartitionSpec as P

MESH = pl.DeviceIdType.MESH
EPSILON = 1e-06
MASKED = -1e30
F32 = jnp.float32
BF16 = jnp.bfloat16
WIDTH = 3072
ROWS = 128
COLS = 384
HEAD = 128
GROUP = 3
PIECE = 96
SCORE_SCALE = HEAD ** (-0.5) * math.log2(math.e)


def rem(a, b):
    return lax.rem(a, jnp.int32(b))


def div(a, b):
    return lax.div(a, jnp.int32(b))


def dot(a, b):
    return jnp.dot(a, b, preferred_element_type=F32)


def dot_t(a, b):
    return lax.dot_general(a, b, (((1,), (1,)), ((), ())), preferred_element_type=F32)


def kernel(
    window_ref,
    blocks_ref,
    tokens_ref,
    gains_ref,
    sq_hbm,
    skv_hbm,
    so_hbm,
    shkv_hbm,
    cq_hbm,
    co_hbm,
    out_ref,
    sq,
    skv,
    so,
    shkv,
    wall,
    xg,
    rs,
    ob,
    xs,
    acc,
    ssq,
    qs,
    ctx,
    halo,
    kc,
    vc,
    sc,
    mx,
    den,
    oacc,
    load_sem,
    own_sem,
    ag_send,
    ag_recv,
    rs_send,
    rs_recv,
    halo_send,
    halo_recv,
    wz_send,
    wz_recv,
    wx_send,
    wx_recv,
    ws_send,
    ws_recv,
    cz_send,
    cz_recv,
    cx_send,
    cx_recv,
    cs_send,
    cs_recv,
):
    seq = lax.axis_index("seq")
    head = lax.axis_index("head")
    core = rem(seq, 2)
    xp = rem(div(seq, 2), 4)
    zh = div(seq, 8)
    yp = div(head, 2)
    zl = rem(head, 2)

    def seq_at(zz, xx, cc):
        return zz * 8 + xx * 2 + cc

    def head_to(k):
        return rem(yp + div(k, 2), 4) * 2 + rem(zl + rem(k, 2), 2)

    def head_from(k):
        return rem(yp + 4 - div(k, 2), 4) * 2 + rem(zl + rem(k, 2), 2)

    z_to = [rem(zh + d, 4) for d in (1, 2, 3)]
    z_from = [rem(zh + 4 - d, 4) for d in (1, 2, 3)]
    x_to = [rem(xp + d, 4) for d in (1, 2, 3)]
    x_from = [rem(xp + 4 - d, 4) for d in (1, 2, 3)]
    sibling = seq_at(zh, xp, 1 - core)
    following = rem(seq + 1, 32)
    previous = rem(seq + 31, 32)

    loads = [
        pltpu.make_async_copy(a, b, load_sem.at[i])
        for i, (a, b) in enumerate(((sq_hbm, sq), (skv_hbm, skv), (so_hbm, so), (shkv_hbm, shkv)))
    ]
    for copy in loads:
        copy.start()

    def piece_source(p):
        return (cq_hbm if p % 2 == 0 else co_hbm).at[p // 2]

    owns = [
        pltpu.make_async_copy(piece_source(p), wall.at[p, zh, xp, core], own_sem.at[p])
        for p in range(6)
    ]
    for copy in owns:
        copy.start()

    barrier = pltpu.get_barrier_semaphore()

    def greet(s, h):
        pl.semaphore_signal(barrier, inc=1, device_id=(s, h), device_id_type=MESH)

    for k in range(1, 8):
        greet(seq, head_to(jnp.int32(k)))
    for zz in z_to:
        greet(seq_at(zz, xp, core), head)
    for xx in x_to:
        greet(seq_at(zh, xx, core), head)
    greet(sibling, head)
    greet(following, head)
    greet(previous, head)
    pl.semaphore_wait(barrier, 16)

    def remote(src, dst, send, recv, s, h):
        return pltpu.make_async_remote_copy(
            src_ref=src, dst_ref=dst, send_sem=send, recv_sem=recv, device_id=(s, h), device_id_type=MESH
        )

    def ag_out(k, src):
        return remote(src, xg.at[head], ag_send.at[k], ag_recv.at[k], seq, head_to(k))

    def ag_in(k):
        return remote(xg.at[head], xg.at[head_from(k)], ag_send.at[k], ag_recv.at[k], seq, head_to(k))

    def ag_start(src):
        def step(k, carry):
            ag_out(k, src).start()
            return carry

        lax.fori_loop(1, 8, step, 0)

    def ag_drain(src):
        def step(k, carry):
            ag_out(k, src).wait_send()
            return carry

        lax.fori_loop(1, 8, step, 0)

    def rs_copy(k):
        return remote(ob.at[k], rs.at[k], rs_send.at[k], rs_recv.at[k], seq, head_to(k))

    def wz_out(p, i):
        return remote(
            piece_source(p), wall.at[p, zh, xp, core], wz_send.at[p, i], wz_recv.at[p, i],
            seq_at(z_to[i], xp, core), head,
        )

    def wz_in(p, i):
        return remote(
            piece_source(p), wall.at[p, z_from[i], xp, core], wz_send.at[p, i], wz_recv.at[p, i],
            seq_at(z_to[i], xp, core), head,
        )

    def wx_out(p, i):
        part = wall.at[p, :, xp, core]
        return remote(part, part, wx_send.at[p, i], wx_recv.at[p, i], seq_at(zh, x_to[i], core), head)

    def wx_in(p, i):
        part = wall.at[p, :, x_from[i], core]
        return remote(part, part, wx_send.at[p, i], wx_recv.at[p, i], seq_at(zh, x_to[i], core), head)

    def ws_out(p):
        part = wall.at[p, :, :, core]
        return remote(part, part, ws_send.at[p], ws_recv.at[p], sibling, head)

    def ws_in(p):
        part = wall.at[p, :, :, 1 - core]
        return remote(part, part, ws_send.at[p], ws_recv.at[p], sibling, head)

    def weight_z(p):
        for i in range(3):
            wz_out(p, i).start()

    def weight_x(p):
        owns[p].wait()
        for i in range(3):
            wz_in(p, i).wait_recv()
        for i in range(3):
            wx_out(p, i).start()

    def weight_s(p):
        for i in range(3):
            wx_in(p, i).wait_recv()
        ws_out(p).start()

    def weight_wait(p):
        ws_in(p).wait_recv()

    cache = (kc, vc)

    def cz_out(c, i):
        part = cache[c].at[zh, xp, core]
        return remote(part, part, cz_send.at[c, i], cz_recv.at[c, i], seq_at(z_to[i], xp, core), head)

    def cz_in(c, i):
        part = cache[c].at[z_from[i], xp, core]
        return remote(part, part, cz_send.at[c, i], cz_recv.at[c, i], seq_at(z_to[i], xp, core), head)

    def cx_out(c, i):
        part = cache[c].at[:, xp, core]
        return remote(part, part, cx_send.at[c, i], cx_recv.at[c, i], seq_at(zh, x_to[i], core), head)

    def cx_in(c, i):
        part = cache[c].at[:, x_from[i], core]
        return remote(part, part, cx_send.at[c, i], cx_recv.at[c, i], seq_at(zh, x_to[i], core), head)

    def cs_out(c):
        part = cache[c].at[:, :, core]
        return remote(part, part, cs_send.at[c], cs_recv.at[c], sibling, head)

    def cs_in(c):
        part = cache[c].at[:, :, 1 - core]
        return remote(part, part, cs_send.at[c], cs_recv.at[c], sibling, head)

    def gain(row, j):
        return gains_ref[row : row + 1, pl.ds(pl.multiple_of(j * COLS, 128), COLS)]

    def rows_of(j):
        return pl.ds(pl.multiple_of(j * COLS, 128), COLS)

    def square_sum(xf):
        sq2 = xf * xf
        return sq2[:, :HEAD] + sq2[:, HEAD : 2 * HEAD] + sq2[:, 2 * HEAD :]

    def row_factor():
        return lax.rsqrt(jnp.sum(ssq[...], axis=1, keepdims=True) / WIDTH + EPSILON)

    def query_block(p, j):
        w = wall[p, div(j, 2), pl.ds(rem(j, 2) * 2, 2)]
        return w.reshape(COLS, COLS)

    def stack_query(factor):
        for g in range(GROUP):
            part = acc[:, g * HEAD : (g + 1) * HEAD]
            qs[g * HEAD : (g + 1) * HEAD, :] = (part * (factor * SCORE_SCALE)).astype(BF16)

    def spread_context():
        inv = 1.0 / jnp.sum(den[...], axis=1, keepdims=True)
        c = (oacc[...] * inv).astype(BF16)
        for g in range(GROUP):
            ctx[:, g * HEAD : (g + 1) * HEAD] = c[g * HEAD : (g + 1) * HEAD, :]

    def reduce_out(block_of):
        def step(k, carry):
            ob[k] = block_of(head_to(k)).astype(BF16)
            rs_copy(k).start()
            return carry

        lax.fori_loop(1, 8, step, 0)
        xs[...] += block_of(head).astype(BF16).astype(F32)

    def reduce_in():
        def step(k, carry):
            rs_copy(k).wait_recv()
            xs[...] += rs[k].astype(F32)
            return carry

        lax.fori_loop(1, 8, step, 0)

    def rs_drain():
        def step(k, carry):
            rs_copy(k).wait_send()
            return carry

        lax.fori_loop(1, 8, step, 0)

    ag_start(tokens_ref)
    weight_z(0)
    xg[head] = tokens_ref[...]
    xs[...] = tokens_ref[...].astype(F32)
    acc[...] = jnp.zeros_like(acc)
    ssq[...] = jnp.zeros_like(ssq)
    loads[0].wait()
    loads[1].wait()

    def first_block(j):
        xf = xg[j].astype(F32)
        ssq[...] += square_sum(xf)
        hb = (xf * gain(0, j)).astype(BF16)
        acc[:, COLS : COLS + HEAD] += dot(hb, skv[0, rows_of(j)])
        acc[:, COLS + HEAD :] += dot(hb, skv[1, rows_of(j)])
        acc[:, :COLS] += dot(hb, sq[rows_of(j)])

    first_block(head)

    def first_step(k, carry):
        ag_in(k).wait_recv()
        first_block(head_from(k))
        return carry

    lax.fori_loop(1, 8, first_step, 0)
    factor = row_factor()
    halo[0] = (acc[:, COLS : COLS + HEAD] * factor).astype(BF16)
    halo[1] = (acc[:, COLS + HEAD :] * factor).astype(BF16)
    halo_copy = remote(halo.at[pl.ds(0, 2)], halo.at[pl.ds(2, 2)], halo_send, halo_recv, following, head)
    halo_copy.start()
    weight_z(1)
    stack_query(factor)
    ag_drain(tokens_ref)
    weight_x(0)

    row = lax.broadcasted_iota(jnp.int32, (ROWS, 1), 0)
    col = lax.broadcasted_iota(jnp.int32, (1, 2 * ROWS), 1)
    offset = row + ROWS - col
    present = (offset >= 0) & (col >= jnp.where(seq == 0, ROWS, 0))
    loads[2].wait()
    halo_copy.wait_recv()
    for g in range(GROUP):
        here = slice(g * HEAD, (g + 1) * HEAD)
        qg = qs[here, :]
        near = jnp.concatenate([dot_t(qg, halo[2]), dot_t(qg, halo[0])], axis=1)
        near = jnp.where(present & (offset < window_ref[g]), near, MASKED)
        top = jnp.max(near, axis=1, keepdims=True)
        weights = jnp.exp2(near - top)
        den[here, :] = weights[:, :ROWS] + weights[:, ROWS:]
        wb = weights.astype(BF16)
        oacc[here, :] = dot(wb[:, :ROWS], halo[3]) + dot(wb[:, ROWS:], halo[1])
    spread_context()
    cvals = ctx[...]
    reduce_out(lambda j: dot(cvals, so[:, pl.ds(pl.multiple_of(j * COLS, 128), COLS)]))
    weight_z(2)
    weight_x(1)
    weight_s(0)
    reduce_in()
    xg[head] = xs[...].astype(BF16)
    own = xg.at[head]
    ag_start(own)
    weight_z(3)
    rs_drain()

    acc[...] = jnp.zeros_like(acc)
    ssq[...] = jnp.zeros_like(ssq)
    loads[3].wait()

    def cache_block(j):
        xf = xg[j].astype(F32)
        ssq[...] += square_sum(xf)
        hb = (xf * gain(1, j)).astype(BF16)
        acc[:, COLS : COLS + HEAD] += dot(hb, shkv[0, rows_of(j)])
        acc[:, COLS + HEAD :] += dot(hb, shkv[1, rows_of(j)])

    cache_block(head)

    def cache_step(k, carry):
        ag_in(k).wait_recv()
        cache_block(head_from(k))
        return carry

    lax.fori_loop(1, 8, cache_step, 0)
    factor = row_factor()
    kc[zh, xp, core] = (acc[:, COLS : COLS + HEAD] * factor).astype(BF16)
    for i in range(3):
        cz_out(0, i).start()
    vc[zh, xp, core] = (acc[:, COLS + HEAD :] * factor).astype(BF16)
    for i in range(3):
        cz_out(1, i).start()
    weight_s(1)
    weight_wait(0)

    def query0_step(j, carry):
        hb = (xg[j].astype(F32) * gain(2, j)).astype(BF16)
        acc[:, :COLS] += dot(hb, query_block(0, j))
        return carry

    lax.fori_loop(0, 8, query0_step, 0)
    stack_query(factor)
    for c in range(2):
        for i in range(3):
            cz_in(c, i).wait_recv()
        for i in range(3):
            cx_out(c, i).start()
    weight_x(2)
    weight_z(4)
    for c in range(2):
        for i in range(3):
            cx_in(c, i).wait_recv()
        cs_out(c).start()
    ag_drain(own)

    tall_row = rem(lax.broadcasted_iota(jnp.int32, (GROUP * ROWS, 1), 0), ROWS)
    causal_col = jnp.where(col < ROWS, col, -1)

    for section in range(3):
        if section > 0:
            ag_start(own)
            rs_drain()
            if section == 1:
                weight_z(5)
                weight_x(4)
                weight_s(3)
            else:
                weight_s(5)
            acc[...] = jnp.zeros_like(acc)
            ssq[...] = jnp.zeros_like(ssq)
            weight_wait(2 * section)

            def query_block_step(j, section=section):
                xf = xg[j].astype(F32)
                ssq[...] += square_sum(xf)
                hb = (xf * gain(2 + section, j)).astype(BF16)
                acc[:, :COLS] += dot(hb, query_block(2 * section, j))

            query_block_step(head)

            def query_step(k, carry, query_block_step=query_block_step):
                ag_in(k).wait_recv()
                query_block_step(head_from(k))
                return carry

            lax.fori_loop(1, 8, query_step, 0)
            stack_query(row_factor())
            ag_drain(own)

        if section == 0:
            cs_in(0).wait_recv()
        qv = qs[...]
        mx[...] = jnp.full_like(mx, MASKED)

        def pick(ref, i):
            n = jnp.maximum(blocks_ref[section, 0, i], 0)
            return ref[div(n, 8), rem(div(n, 2), 4), rem(n, 2)]

        def score_step(i, carry, qv=qv, pick=pick, section=section):
            keys = jnp.concatenate([pick(kc, 2 * i), pick(kc, 2 * i + 1)], axis=0)
            t = dot_t(qv, keys)
            low = jnp.where(blocks_ref[section, 0, 2 * i] >= 0, 0.0, MASKED)
            high = jnp.where(blocks_ref[section, 0, 2 * i + 1] >= 0, 0.0, MASKED)
            bias = jnp.where(col < ROWS, low, high)
            t = jnp.where(causal_col <= tall_row + jnp.where(i == 0, 0, 4096), t, MASKED) + bias
            sc[i] = t
            mx[...] = jnp.maximum(mx[...], jnp.maximum(t[:, :HEAD], t[:, HEAD:]))
            return carry

        lax.fori_loop(0, 8, score_step, 0)
        top = jnp.max(mx[...], axis=1, keepdims=True)
        den[...] = jnp.zeros_like(den)
        oacc[...] = jnp.zeros_like(oacc)
        if section == 0:
            cs_in(1).wait_recv()

        def value_step(i, carry, top=top, pick=pick):
            weights = jnp.exp2(sc[i] - top)
            den[...] += weights[:, :HEAD] + weights[:, HEAD:]
            values = jnp.concatenate([pick(vc, 2 * i), pick(vc, 2 * i + 1)], axis=0)
            oacc[...] += dot(weights.astype(BF16), values)
            return carry

        lax.fori_loop(0, 8, value_step, 0)
        spread_context()
        weight_wait(2 * section + 1)
        cvals = ctx[...]
        reduce_out(lambda j, cvals=cvals, section=section: dot_t(cvals, query_block(2 * section + 1, j)))
        if section == 0:
            weight_x(3)
            weight_s(2)
        elif section == 1:
            weight_x(5)
            weight_s(4)
        reduce_in()
        if section < 2:
            xg[head] = xs[...].astype(BF16)
    out_ref[...] = xs[...]

    rs_drain()
    halo_copy.wait_send()
    for p in range(6):
        for i in range(3):
            wz_out(p, i).wait_send()
            wx_out(p, i).wait_send()
        ws_out(p).wait_send()
    for c in range(2):
        for i in range(3):
            cz_out(c, i).wait_send()
            cx_out(c, i).wait_send()
        cs_out(c).wait_send()


def body(
    tokens,
    norm_gains,
    window,
    self_query,
    self_key_value,
    self_output,
    shared_key_value,
    cross_query,
    cross_output,
    key_blocks,
):
    vmem = pl.BlockSpec(memory_space=pltpu.VMEM)
    smem = pl.BlockSpec(memory_space=pltpu.SMEM)
    hbm = pl.BlockSpec(memory_space=pl.ANY)
    dma = pltpu.SemaphoreType.DMA
    return pl.pallas_call(
        kernel,
        out_shape=jax.ShapeDtypeStruct((ROWS, COLS), F32),
        in_specs=[smem, smem, vmem, vmem] + [hbm] * 6,
        out_specs=vmem,
        scratch_shapes=[
            pltpu.VMEM((WIDTH, COLS), BF16),
            pltpu.VMEM((2, WIDTH, HEAD), BF16),
            pltpu.VMEM((COLS, WIDTH), BF16),
            pltpu.VMEM((2, WIDTH, HEAD), BF16),
            pltpu.VMEM((6, 4, 4, 2, PIECE, COLS), BF16),
            pltpu.VMEM((8, ROWS, COLS), BF16),
            pltpu.VMEM((8, ROWS, COLS), BF16),
            pltpu.VMEM((8, ROWS, COLS), BF16),
            pltpu.VMEM((ROWS, COLS), F32),
            pltpu.VMEM((ROWS, COLS + 2 * HEAD), F32),
            pltpu.VMEM((ROWS, HEAD), F32),
            pltpu.VMEM((GROUP * ROWS, HEAD), BF16),
            pltpu.VMEM((ROWS, COLS), BF16),
            pltpu.VMEM((4, ROWS, HEAD), BF16),
            pltpu.VMEM((4, 4, 2, ROWS, HEAD), BF16),
            pltpu.VMEM((4, 4, 2, ROWS, HEAD), BF16),
            pltpu.VMEM((8, GROUP * ROWS, 2 * HEAD), F32),
            pltpu.VMEM((GROUP * ROWS, HEAD), F32),
            pltpu.VMEM((GROUP * ROWS, HEAD), F32),
            pltpu.VMEM((GROUP * ROWS, HEAD), F32),
            dma((4,)),
            dma((6,)),
            dma((8,)),
            dma((8,)),
            dma((8,)),
            dma((8,)),
            dma,
            dma,
            dma((6, 3)),
            dma((6, 3)),
            dma((6, 3)),
            dma((6, 3)),
            dma((6,)),
            dma((6,)),
            dma((2, 3)),
            dma((2, 3)),
            dma((2, 3)),
            dma((2, 3)),
            dma((2,)),
            dma((2,)),
        ],
        compiler_params=pltpu.CompilerParams(
            collective_id=0, has_side_effects=True, vmem_limit_bytes=60 * 1024 * 1024
        ),
        name="window",
    )(
        window,
        key_blocks,
        tokens,
        norm_gains,
        self_query,
        self_key_value,
        self_output,
        shared_key_value,
        cross_query,
        jnp.swapaxes(cross_output, 1, 2),
    )


def solution(mesh):
    placed = (
        P("seq", "head"),
        P(),
        P("head"),
        P(None, "head"),
        P(None, None, "head"),
        P("head", None),
        P(None, None, "head"),
        P(None, "seq", "head"),
        P(None, "head", "seq"),
        P(None, "seq", None),
    )
    return jax.shard_map(
        body, mesh=mesh, in_specs=placed, out_specs=P("seq", "head"), check_vma=False
    )
```

time: 705 us -> 159 us (0.23)
  the two profiles are of different devices: /device:TPU:4 before, /device:TPU:1 now
where the time goes in v1:
time: 159 us
  Pallas kernels  157 us (99%)
  local copies, waits for them, and re-layouts  1.62 us (1%)
    pallas_call x1, Pallas kernels, body(): pl.pallas_call(kernel, out_shape=jax.ShapeDtypeStruct((ROWS, COLS), F32),...  157 us

profile of v1, /device:TPU:1, one launch (start us, length us, event | category | flops | bytes accessed | tf_op | source)
XLA Modules:
  0.0 159.1 jit_solution(14308493373249083839)
XLA Ops:
  0.0 157.5 %window.1 = f32[128,384]{1,0:T(8,128)} custom-call(s32[3]{0:T(128)} %window_ref.1, s32[3,1,16]{2,1,0:T(1,128)} %blocks_ref.1, bf16[128,384]{1,0:T(8,128)(2,1)} %tokens_ref.1, f32[5,3072]{1,0:T(8,128)} %gains_ref.1, bf16[3072,384]{1,0:T(8,128)(2,1)} %sq_hbm.1, bf16[2,3072,128]{2,1,0:T(8,128)(2,1)} %skv_hbm.1, bf16[384,3072]{1,0:T(8,128)(2,1)} %so_hbm.1, ...), custom_call_target="tpu_custom_call" | custom-call | tf_op jit(solution)/shard_map/window/pallas_call | solution.py:531
  157.5 1.6 %copy.12 = f32[128,384]{1,0:T(8,128)} copy(f32[128,384]{1,0:T(8,128)} %window.1) | data formatting | bytes 393216

commit v2 on v1

v2 whole, which is shorter than its diff:
```python
import math

import jax
import jax.numpy as jnp
from jax import lax
from jax.experimental import pallas as pl
from jax.experimental.pallas import tpu as pltpu
from jax.sharding import PartitionSpec as P

MESH = pl.DeviceIdType.MESH
EPSILON = 1e-06
MASKED = -1e30
F32 = jnp.float32
BF16 = jnp.bfloat16
WIDTH = 3072
ROWS = 128
COLS = 384
HEAD = 128
GROUP = 3
PIECE = 96
HALF = 64
SCORE_SCALE = HEAD ** (-0.5) * math.log2(math.e)


mark = jax.named_scope


def rem(a, b):
    return lax.rem(a, jnp.int32(b))


def div(a, b):
    return lax.div(a, jnp.int32(b))


def dot(a, b):
    return jnp.dot(a, b, preferred_element_type=F32)


def dot_t(a, b):
    return lax.dot_general(a, b, (((1,), (1,)), ((), ())), preferred_element_type=F32)


def kernel(
    window_ref,
    blocks_ref,
    tokens_hbm,
    gains_hbm,
    sq_hbm,
    skv_hbm,
    so_hbm,
    shkv_hbm,
    cq_hbm,
    co_hbm,
    out_ref,
    gains_ref,
    sq,
    skv,
    so,
    shkv,
    wall,
    xg,
    rs,
    ob,
    xs,
    acc,
    qs,
    ctx,
    own_kv,
    halo,
    kc,
    vc,
    sc,
    den,
    oacc,
    load_sem,
    own_sem,
    ag_send,
    ag_recv,
    rs_send,
    rs_recv,
    halo_send,
    halo_recv,
    wz_send,
    wz_recv,
    wx_send,
    wx_recv,
    wy_send,
    wy_recv,
    ws_send,
    ws_recv,
    cz_send,
    cz_recv,
    cx_send,
    cx_recv,
    cs_send,
    cs_recv,
):
    seq = lax.axis_index("seq")
    head = lax.axis_index("head")
    core = rem(seq, 2)
    xp = rem(div(seq, 2), 4)
    zh = div(seq, 8)
    yp = div(head, 2)
    zl = rem(head, 2)

    def seq_at(zz, xx, cc):
        return zz * 8 + xx * 2 + cc

    def head_to(k):
        return rem(yp + div(k, 2), 4) * 2 + rem(zl + rem(k, 2), 2)

    def head_from(k):
        return rem(yp + 4 - div(k, 2), 4) * 2 + rem(zl + rem(k, 2), 2)

    z_to = [rem(zh + d, 4) for d in (1, 2, 3)]
    z_from = [rem(zh + 4 - d, 4) for d in (1, 2, 3)]
    x_to = [rem(xp + d, 4) for d in (1, 2, 3)]
    x_from = [rem(xp + 4 - d, 4) for d in (1, 2, 3)]
    sibling = seq_at(zh, xp, 1 - core)
    following = rem(seq + 1, 32)
    previous = rem(seq + 31, 32)

    def rows_half(h):
        return pl.ds(h * HALF, HALF)

    barrier = pltpu.get_barrier_semaphore()

    def greet(s, h):
        pl.semaphore_signal(barrier, inc=1, device_id=(s, h), device_id_type=MESH)

    for zz in z_to:
        greet(seq_at(zz, xp, core), head)
    for k in range(1, 8):
        greet(seq, head_to(jnp.int32(k)))
    for xx in x_to:
        greet(seq_at(zh, xx, core), head)
    greet(sibling, head)
    greet(following, head)
    greet(previous, head)

    loads = [
        pltpu.make_async_copy(a, b, load_sem.at[i])
        for i, (a, b) in enumerate(
            (
                (tokens_hbm.at[rows_half(0)], xg.at[0, head]),
                (tokens_hbm.at[rows_half(1)], xg.at[1, head]),
                (gains_hbm, gains_ref),
                (skv_hbm, skv),
                (sq_hbm, sq),
                (so_hbm, so),
                (shkv_hbm, shkv),
            )
        )
    ]
    for copy in loads:
        copy.start()

    def piece_source(p):
        return (cq_hbm if p % 2 == 0 else co_hbm).at[p // 2]

    owns = [
        pltpu.make_async_copy(piece_source(p), wall.at[p, zh, xp, core], own_sem.at[p])
        for p in range(6)
    ]
    for copy in owns:
        copy.start()

    with mark("barrier"):
        pl.semaphore_wait(barrier, 16)

    def remote(src, dst, send, recv, s, h):
        return pltpu.make_async_remote_copy(
            src_ref=src, dst_ref=dst, send_sem=send, recv_sem=recv, device_id=(s, h), device_id_type=MESH
        )

    beside_z = yp * 2 + 1 - zl

    def ag_out(h, k, src):
        return remote(src, xg.at[h, head], ag_send.at[h, k], ag_recv.at[h, k], seq, head_to(jnp.int32(k)))

    def ag_pass(h, k):
        part = xg.at[h, beside_z]
        return remote(part, part, ag_send.at[h, k], ag_recv.at[h, k], seq, head_to(jnp.int32(k - 1)))

    def ag_in(h, k):
        return remote(
            xg.at[h, head], xg.at[h, head_from(jnp.int32(k))], ag_send.at[h, k], ag_recv.at[h, k], seq,
            head_to(jnp.int32(k)),
        )

    def ag_start(h, src):
        for k in (1, 2, 6, 4):
            ag_out(h, k, src).start()

    def ag_forward(h):
        with mark("forward"):
            ag_in(h, 1).wait_recv()
            for k in (3, 7, 5):
                ag_pass(h, k).start()

    def ag_near(h):
        for k in (2, 6, 4):
            ag_in(h, k).wait_recv()

    def ag_far(h):
        for k in (3, 7, 5):
            ag_in(h, k).wait_recv()

    def ag_drain(h, src):
        for k in (1, 2, 6, 4):
            ag_out(h, k, src).wait_send()
        for k in (3, 7, 5):
            ag_pass(h, k).wait_send()

    def rs_copy(h, k):
        to = head_to(jnp.int32(k))
        return remote(ob.at[h, to], rs.at[h, k], rs_send.at[h, k], rs_recv.at[h, k], seq, to)

    def wz_out(p, i):
        return remote(
            piece_source(p), wall.at[p, zh, xp, core], wz_send.at[p, i], wz_recv.at[p, i],
            seq_at(z_to[i], xp, core), head,
        )

    def wz_in(p, i):
        return remote(
            piece_source(p), wall.at[p, z_from[i], xp, core], wz_send.at[p, i], wz_recv.at[p, i],
            seq_at(z_to[i], xp, core), head,
        )

    beside = (x_to[0], x_to[2])

    def wx_out(p, i):
        part = wall.at[p, :, xp, core]
        return remote(part, part, wx_send.at[p, i], wx_recv.at[p, i], seq_at(zh, beside[i], core), head)

    def wx_in(p, i):
        part = wall.at[p, :, beside[1 - i], core]
        return remote(part, part, wx_send.at[p, i], wx_recv.at[p, i], seq_at(zh, beside[i], core), head)

    def wy_out(p, i):
        part = wall.at[p, pl.ds(2 * i, 2), beside[1 - i], core]
        return remote(part, part, wy_send.at[p, i], wy_recv.at[p, i], seq_at(zh, beside[i], core), head)

    def wy_in(p, i):
        part = wall.at[p, pl.ds(2 * i, 2), x_to[1], core]
        return remote(part, part, wy_send.at[p, i], wy_recv.at[p, i], seq_at(zh, beside[i], core), head)

    def ws_out(p):
        part = wall.at[p, :, :, core]
        return remote(part, part, ws_send.at[p], ws_recv.at[p], sibling, head)

    def ws_in(p):
        part = wall.at[p, :, :, 1 - core]
        return remote(part, part, ws_send.at[p], ws_recv.at[p], sibling, head)

    def weight_z(p):
        for i in range(3):
            wz_out(p, i).start()

    def weight_x(p):
        with mark("weight_x"):
            owns[p].wait()
            for i in range(3):
                wz_in(p, i).wait_recv()
            for i in range(2):
                wx_out(p, i).start()

    def weight_y(p):
        with mark("weight_y"):
            for i in range(2):
                wx_in(p, i).wait_recv()
                wy_out(p, i).start()

    def weight_s(p):
        with mark("weight_s"):
            for i in range(2):
                wy_in(p, i).wait_recv()
            ws_out(p).start()

    def weight_wait(p):
        with mark("weight_wait"):
            ws_in(p).wait_recv()

    cache = (kc, vc)

    def cz_part(c, h, zz):
        return cache[c].at[zz, xp, core, rows_half(h)]

    def cz_out(c, h, i):
        part = cz_part(c, h, zh)
        return remote(part, part, cz_send.at[c, h, i], cz_recv.at[c, h, i], seq_at(z_to[i], xp, core), head)

    def cz_in(c, h, i):
        part = cz_part(c, h, z_from[i])
        return remote(part, part, cz_send.at[c, h, i], cz_recv.at[c, h, i], seq_at(z_to[i], xp, core), head)

    def cx_out(c, h, m, i):
        part = cz_part(c, h, rem(zh + 4 - m, 4))
        return remote(part, part, cx_send.at[c, h, m, i], cx_recv.at[c, h, m, i], seq_at(zh, x_to[i], core), head)

    def cx_in(c, h, m, i):
        part = cache[c].at[rem(zh + 4 - m, 4), x_from[i], core, rows_half(h)]
        return remote(part, part, cx_send.at[c, h, m, i], cx_recv.at[c, h, m, i], seq_at(zh, x_to[i], core), head)

    def cs_out(c, h):
        part = cache[c].at[:, :, core, rows_half(h)]
        return remote(part, part, cs_send.at[c, h], cs_recv.at[c, h], sibling, head)

    def cs_in(c, h):
        part = cache[c].at[:, :, 1 - core, rows_half(h)]
        return remote(part, part, cs_send.at[c, h], cs_recv.at[c, h], sibling, head)

    def cols_of(j):
        return pl.ds(pl.multiple_of(j * COLS, 128), COLS)

    def gain(row, j):
        return gains_ref[row : row + 1, cols_of(j)]

    def square_sum(xf):
        sq2 = xf * xf
        return sq2[:, :HEAD] + sq2[:, HEAD : 2 * HEAD] + sq2[:, 2 * HEAD :]

    def row_factor(squares):
        return lax.rsqrt(jnp.sum(squares, axis=1, keepdims=True) / WIDTH + EPSILON)

    def plane(h, zz, row):
        parts, squares = [], 0.0
        for y in range(4):
            j = y * 2 + zz
            xf = xg[h, j].astype(F32)
            squares = squares + square_sum(xf)
            parts.append((xf * gain(row, j)).astype(BF16))
        return jnp.concatenate(parts, axis=1), squares

    def key_value_rows(ref, zz):
        keys = jnp.concatenate([ref[0, cols_of(y * 2 + zz)] for y in range(4)], axis=0)
        values = jnp.concatenate([ref[1, cols_of(y * 2 + zz)] for y in range(4)], axis=0)
        return jnp.concatenate([keys, values], axis=1)

    def piece_rows(p, zz):
        return wall[p, :, pl.ds(zz * 2, 2)].reshape(4 * COLS, COLS)

    def stack_query(h, full, factor):
        scaled = full * (factor * SCORE_SCALE)
        for g in range(GROUP):
            qs[h, g * HALF : (g + 1) * HALF, :] = scaled[:, g * HEAD : (g + 1) * HEAD].astype(BF16)

    def spread_context():
        inv = 1.0 / jnp.sum(den[...], axis=1, keepdims=True)
        c = (oacc[...] * inv).astype(BF16)
        for g in range(GROUP):
            ctx[:, g * HEAD : (g + 1) * HEAD] = c[g * HALF : (g + 1) * HALF, :]

    far = (3, 7, 5, 1)
    near = (4, 2, 6)

    def reduce_out(h, plane_of):
        with mark("rs_out"):
            for zz, ks in ((1 - zl, far), (zl, near)):
                for y, block in enumerate(plane_of(zz)):
                    ob[h, y * 2 + zz] = block.astype(BF16)
                for k in ks:
                    rs_copy(h, k).start()

    def reduce_in(h):
        with mark("rs_in"):
            for k in near + far:
                rs_copy(h, k).wait_recv()
            total = xs[h] + ob[h, head].astype(F32)
            for k in near + far:
                total = total + rs[h, k].astype(F32)
        return total

    def rs_drain(h):
        for k in near + far:
            rs_copy(h, k).wait_send()

    def own_part(h):
        return xg.at[h, head]

    for h in range(2):
        ag_start(h, tokens_hbm.at[rows_half(h)])
    weight_z(0)
    for h in range(2):
        ag_forward(h)
    weight_z(1)
    for copy in loads[:5]:
        copy.wait()

    def halo_of(h):
        return remote(
            own_kv.at[:, rows_half(h)], halo.at[:, rows_half(h)], halo_send.at[h], halo_recv.at[h], following, head
        )

    for h in range(2):
        xs[h] = xg[h, head].astype(F32)
        with mark("ag0"):
            ag_near(h)
            hb, squares = plane(h, zl, 0)
            acc[:, COLS:] = dot(hb, key_value_rows(skv, zl))
            acc[:, :COLS] = dot(hb, jnp.concatenate([sq[cols_of(y * 2 + zl)] for y in range(4)], axis=0))
            ag_far(h)
            hb, more = plane(h, 1 - zl, 0)
            factor = row_factor(squares + more)
            kv = (acc[:, COLS:] + dot(hb, key_value_rows(skv, 1 - zl))) * factor
            own_kv[0, rows_half(h)] = kv[:, :HEAD].astype(BF16)
            own_kv[1, rows_half(h)] = kv[:, HEAD:].astype(BF16)
            halo_of(h).start()
            full = acc[:, :COLS] + dot(
                hb, jnp.concatenate([sq[cols_of(y * 2 + 1 - zl)] for y in range(4)], axis=0)
            )
            stack_query(h, full, factor)

    weight_z(2)
    for h in range(2):
        ag_drain(h, tokens_hbm.at[rows_half(h)])

    col = lax.broadcasted_iota(jnp.int32, (1, 2 * ROWS), 1)
    loads[5].wait()
    with mark("halo"):
        for h in range(2):
            halo_of(h).wait_recv()
    weight_x(0)
    for h in range(2):
        row = lax.broadcasted_iota(jnp.int32, (HALF, 1), 0) + h * HALF
        offset = row + ROWS - col
        present = (offset >= 0) & (col >= jnp.where(seq == 0, ROWS, 0))
        with mark("self_attn"):
            for g in range(GROUP):
                here = slice(g * HALF, (g + 1) * HALF)
                qg = qs[h, here, :]
                score = jnp.concatenate([dot_t(qg, halo[0]), dot_t(qg, own_kv[0])], axis=1)
                score = jnp.where(present & (offset < window_ref[g]), score, MASKED)
                top = jnp.max(score, axis=1, keepdims=True)
                weights = jnp.exp2(score - top)
                den[here, :] = weights[:, :ROWS] + weights[:, ROWS:]
                wb = weights.astype(BF16)
                oacc[here, :] = dot(wb[:, :ROWS], halo[1]) + dot(wb[:, ROWS:], own_kv[1])
            spread_context()
        cvals = ctx[...]
        reduce_out(h, lambda zz, cvals=cvals: [dot(cvals, so[:, cols_of(y * 2 + zz)]) for y in range(4)])
    weight_y(0)
    weight_x(1)
    for h in range(2):
        total = reduce_in(h)
        xs[h] = total
        xg[h, head] = total.astype(BF16)
        ag_start(h, own_part(h))
        if h == 0:
            ag_forward(0)
        else:
            weight_z(3)
            weight_s(0)
    loads[6].wait()

    factors = []
    for h in range(2):
        with mark("ag1"):
            ag_near(h)
            hb, squares = plane(h, zl, 1)
            acc[:, COLS:] = dot(hb, key_value_rows(shkv, zl))
            if h == 0:
                ag_forward(1)
                weight_y(1)
                weight_x(2)
            ag_far(h)
            hb, more = plane(h, 1 - zl, 1)
            factor = row_factor(squares + more)
            kv = (acc[:, COLS:] + dot(hb, key_value_rows(shkv, 1 - zl))) * factor
        factors.append(factor)
        for c in range(2):
            cache[c][zh, xp, core, rows_half(h)] = kv[:, c * HEAD : (c + 1) * HEAD].astype(BF16)
            for i in range(3):
                cz_out(c, h, i).start()
            for i in range(3):
                cx_out(c, h, 0, i).start()
    weight_s(1)
    weight_wait(0)
    for h in range(2):
        rs_drain(h)
        with mark("q0"):
            full = 0.0
            for zz in (0, 1):
                hb, _ = plane(h, zz, 2)
                full = full + dot(hb, piece_rows(0, zz))
        stack_query(h, full, factors[h])
        ag_drain(h, own_part(h))
    with mark("cache_z"):
        for h in range(2):
            for c in range(2):
                for m in (1, 2, 3):
                    cz_in(c, h, m - 1).wait_recv()
                    for i in range(3):
                        cx_out(c, h, m, i).start()
    weight_y(2)
    weight_x(3)
    weight_z(4)
    with mark("cache_x"):
        for h in range(2):
            for c in range(2):
                for m in range(4):
                    for i in range(3):
                        cx_in(c, h, m, i).wait_recv()
                cs_out(c, h).start()
    weight_s(2)
    with mark("cache_s"):
        for h in range(2):
            for c in range(2):
                cs_in(c, h).wait_recv()

    half_row = rem(lax.broadcasted_iota(jnp.int32, (GROUP * HALF, 1), 0), HALF)
    causal_col = jnp.where(col < ROWS, col, -1)

    for section in range(3):
        for h in range(2):
            if section > 0:
                if h == 0:
                    weight_wait(2 * section)
                with mark("ag"):
                    ag_near(h)
                    hb, squares = plane(h, zl, 2 + section)
                    acc[:, :COLS] = dot(hb, piece_rows(2 * section, zl))
                    ag_far(h)
                    hb, more = plane(h, 1 - zl, 2 + section)
                    full = acc[:, :COLS] + dot(hb, piece_rows(2 * section, 1 - zl))
                    stack_query(h, full, row_factor(squares + more))

            qv = qs[h]

            def pick(ref, i, section=section):
                n = jnp.maximum(blocks_ref[section, 0, i], 0)
                return ref[div(n, 8), rem(div(n, 2), 4), rem(n, 2)]

            with mark("score"):
                best = None
                for i in range(8):
                    keys = jnp.concatenate([pick(kc, 2 * i), pick(kc, 2 * i + 1)], axis=0)
                    t = dot_t(qv, keys)
                    low = jnp.where(blocks_ref[section, 0, 2 * i] >= 0, 0.0, MASKED)
                    high = jnp.where(blocks_ref[section, 0, 2 * i + 1] >= 0, 0.0, MASKED)
                    if i == 0:
                        t = jnp.where(causal_col <= half_row + h * HALF, t, MASKED)
                    t = t + jnp.where(col < ROWS, low, high)
                    sc[i] = t
                    pair = jnp.maximum(t[:, :HEAD], t[:, HEAD:])
                    best = pair if best is None else jnp.maximum(best, pair)
                top = jnp.max(best, axis=1, keepdims=True)
            if section > 0:
                if h == 0:
                    ag_forward(1)
                ag_drain(h, own_part(h))

            with mark("value"):
                dens, outs = None, None
                for i in range(8):
                    weights = jnp.exp2(sc[i] - top)
                    part = weights[:, :HEAD] + weights[:, HEAD:]
                    dens = part if dens is None else dens + part
                    values = jnp.concatenate([pick(vc, 2 * i), pick(vc, 2 * i + 1)], axis=0)
                    part = dot(weights.astype(BF16), values)
                    outs = part if outs is None else outs + part
                den[...] = dens
                oacc[...] = outs
            spread_context()
            if h == 0:
                weight_wait(2 * section + 1)
            cvals = ctx[...]
            if section > 0:
                rs_drain(h)

            def plane_of(zz, cvals=cvals, section=section):
                wide = dot_t(cvals, piece_rows(2 * section + 1, zz))
                return [wide[:, y * COLS : (y + 1) * COLS] for y in range(4)]

            reduce_out(h, plane_of)
            if section == 0 and h == 0:
                weight_y(3)
                weight_x(4)
                weight_z(5)
            elif section == 1 and h == 0:
                weight_s(4)
            elif section == 1 and h == 1:
                weight_y(5)
        for h in range(2):
            total = reduce_in(h)
            if section < 2:
                xs[h] = total
                xg[h, head] = total.astype(BF16)
                ag_start(h, own_part(h))
                if h == 0:
                    ag_forward(0)
            else:
                out_ref[rows_half(h), :] = total
            if section == 0 and h == 0:
                weight_s(3)
            elif section == 0 and h == 1:
                weight_y(4)
                weight_x(5)
            elif section == 1 and h == 1:
                weight_s(5)
    for h in range(2):
        rs_drain(h)

    for h in range(2):
        halo_of(h).wait_send()
    for p in range(6):
        for i in range(3):
            wz_out(p, i).wait_send()
        for i in range(2):
            wx_out(p, i).wait_send()
            wy_out(p, i).wait_send()
        ws_out(p).wait_send()
    for c in range(2):
        for h in range(2):
            for i in range(3):
                cz_out(c, h, i).wait_send()
                for m in range(4):
                    cx_out(c, h, m, i).wait_send()
            cs_out(c, h).wait_send()


def body(
    tokens,
    norm_gains,
    window,
    self_query,
    self_key_value,
    self_output,
    shared_key_value,
    cross_query,
    cross_output,
    key_blocks,
):
    vmem = pl.BlockSpec(memory_space=pltpu.VMEM)
    smem = pl.BlockSpec(memory_space=pltpu.SMEM)
    hbm = pl.BlockSpec(memory_space=pl.ANY)
    dma = pltpu.SemaphoreType.DMA
    return pl.pallas_call(
        kernel,
        out_shape=jax.ShapeDtypeStruct((ROWS, COLS), F32),
        in_specs=[smem, smem] + [hbm] * 8,
        out_specs=vmem,
        scratch_shapes=[
            pltpu.VMEM((5, WIDTH), F32),
            pltpu.VMEM((WIDTH, COLS), BF16),
            pltpu.VMEM((2, WIDTH, HEAD), BF16),
            pltpu.VMEM((COLS, WIDTH), BF16),
            pltpu.VMEM((2, WIDTH, HEAD), BF16),
            pltpu.VMEM((6, 4, 4, 2, PIECE, COLS), BF16),
            pltpu.VMEM((2, 8, HALF, COLS), BF16),
            pltpu.VMEM((2, 8, HALF, COLS), BF16),
            pltpu.VMEM((2, 8, HALF, COLS), BF16),
            pltpu.VMEM((2, HALF, COLS), F32),
            pltpu.VMEM((HALF, COLS + 2 * HEAD), F32),
            pltpu.VMEM((2, GROUP * HALF, HEAD), BF16),
            pltpu.VMEM((HALF, COLS), BF16),
            pltpu.VMEM((2, ROWS, HEAD), BF16),
            pltpu.VMEM((2, ROWS, HEAD), BF16),
            pltpu.VMEM((4, 4, 2, ROWS, HEAD), BF16),
            pltpu.VMEM((4, 4, 2, ROWS, HEAD), BF16),
            pltpu.VMEM((8, GROUP * HALF, 2 * HEAD), F32),
            pltpu.VMEM((GROUP * HALF, HEAD), F32),
            pltpu.VMEM((GROUP * HALF, HEAD), F32),
            dma((7,)),
            dma((6,)),
            dma((2, 8)),
            dma((2, 8)),
            dma((2, 8)),
            dma((2, 8)),
            dma((2,)),
            dma((2,)),
            dma((6, 3)),
            dma((6, 3)),
            dma((6, 2)),
            dma((6, 2)),
            dma((6, 2)),
            dma((6, 2)),
            dma((6,)),
            dma((6,)),
            dma((2, 2, 3)),
            dma((2, 2, 3)),
            dma((2, 2, 4, 3)),
            dma((2, 2, 4, 3)),
            dma((2, 2)),
            dma((2, 2)),
        ],
        compiler_params=pltpu.CompilerParams(
            collective_id=0, has_side_effects=True, vmem_limit_bytes=60 * 1024 * 1024
        ),
        name="window",
    )(
        window,
        key_blocks,
        tokens,
        norm_gains,
        self_query,
        self_key_value,
        self_output,
        shared_key_value,
        cross_query,
        jnp.swapaxes(cross_output, 1, 2),
    )


def solution(mesh):
    placed = (
        P("seq", "head"),
        P(),
        P("head"),
        P(None, "head"),
        P(None, None, "head"),
        P("head", None),
        P(None, None, "head"),
        P(None, "seq", "head"),
        P(None, "head", "seq"),
        P(None, "seq", None),
    )
    return jax.shard_map(
        body, mesh=mesh, in_specs=placed, out_specs=P("seq", "head"), check_vma=False
    )
```

time: 159 us -> 139 us (0.87)
  the two profiles are of different devices: /device:TPU:1 before, /device:TPU:4 now
where the time goes in v2:
time: 139 us
  Pallas kernels  138 us (99%)
  local copies, waits for them, and re-layouts  1.62 us (1%)
    pallas_call x1, Pallas kernels, body(): pl.pallas_call(kernel, out_shape=jax.ShapeDtypeStruct((ROWS, COLS), F32),...  138 us

profile of v2, /device:TPU:4, one launch (start us, length us, event | category | flops | bytes accessed | tf_op | source)
XLA Modules:
  0.0 139.3 jit_solution(15517347451259168786)
XLA Ops:
  0.0 137.6 %window.1 = f32[128,384]{1,0:T(8,128)} custom-call(s32[3]{0:T(128)} %window_ref.1, s32[3,1,16]{2,1,0:T(1,128)} %blocks_ref.1, bf16[128,384]{1,0:T(8,128)(2,1)} %tokens_hbm.1, f32[5,3072]{1,0:T(8,128)} %gains_hbm.1, bf16[3072,384]{1,0:T(8,128)(2,1)} %sq_hbm.1, bf16[2,3072,128]{2,1,0:T(8,128)(2,1)} %skv_hbm.1, bf16[384,3072]{1,0:T(8,128)(2,1)} %so_hbm.1, ...), custom_call_target="tpu_custom_call" | custom-call | tf_op jit(solution)/shard_map/window/pallas_call | solution.py:640
  137.7 1.6 %copy.12 = f32[128,384]{1,0:T(8,128)} copy(f32[128,384]{1,0:T(8,128)} %window.1) | data formatting | bytes 393216

commit v3 on v2

--- a/solution.py
+++ b/solution.py
@@ -217,17 +217,30 @@
         to = head_to(jnp.int32(k))
         return remote(ob.at[h, to], rs.at[h, k], rs_send.at[h, k], rs_recv.at[h, k], seq, to)
 
+    beside_zh = (z_to[0], z_to[2])
+    direct = (3,)
+
+    def wz_copy(p, i, src, dst):
+        to = beside_zh[i] if i < 2 else (z_to[1] if p in direct else beside_zh[i - 2])
+        return remote(src, dst, wz_send.at[p, i], wz_recv.at[p, i], seq_at(to, xp, core), head)
+
+    def wz_part(p, i, zz):
+        if i < 2 or p in direct:
+            return wall.at[p, zz, xp, core]
+        return wall.at[p, zz, xp, core, pl.ds((i - 2) * (PIECE // 2), PIECE // 2)]
+
     def wz_out(p, i):
-        return remote(
-            piece_source(p), wall.at[p, zh, xp, core], wz_send.at[p, i], wz_recv.at[p, i],
-            seq_at(z_to[i], xp, core), head,
-        )
+        if i < 2 or p in direct:
+            return wz_copy(p, i, piece_source(p), wz_part(p, i, zh))
+        part = wz_part(p, i, beside_zh[3 - i])
+        return wz_copy(p, i, part, part)
 
     def wz_in(p, i):
-        return remote(
-            piece_source(p), wall.at[p, z_from[i], xp, core], wz_send.at[p, i], wz_recv.at[p, i],
-            seq_at(z_to[i], xp, core), head,
-        )
+        part = wz_part(p, i, beside_zh[1 - i] if i < 2 else z_to[1])
+        return wz_copy(p, i, part, part)
+
+    def wz_steps(p):
+        return (0, 1, 2) if p in direct else (0, 1, 2, 3)
 
     beside = (x_to[0], x_to[2])
 
@@ -256,13 +269,19 @@
         return remote(part, part, ws_send.at[p], ws_recv.at[p], sibling, head)
 
     def weight_z(p):
-        for i in range(3):
+        for i in (0, 1, 2) if p in direct else (0, 1):
             wz_out(p, i).start()
+
+    def weight_f(p):
+        with mark("weight_f"):
+            for i in (0, 1):
+                wz_in(p, i).wait_recv()
+                wz_out(p, i + 2).start()
 
     def weight_x(p):
         with mark("weight_x"):
             owns[p].wait()
-            for i in range(3):
+            for i in (0, 1, 2) if p in direct else (2, 3):
                 wz_in(p, i).wait_recv()
             for i in range(2):
                 wx_out(p, i).start()
@@ -412,8 +431,7 @@
                 hb, jnp.concatenate([sq[cols_of(y * 2 + 1 - zl)] for y in range(4)], axis=0)
             )
             stack_query(h, full, factor)
-
-    weight_z(2)
+        weight_f(h)
     for h in range(2):
         ag_drain(h, tokens_hbm.at[rows_half(h)])
 
@@ -422,7 +440,6 @@
     with mark("halo"):
         for h in range(2):
             halo_of(h).wait_recv()
-    weight_x(0)
     for h in range(2):
         row = lax.broadcasted_iota(jnp.int32, (HALF, 1), 0) + h * HALF
         offset = row + ROWS - col
@@ -441,18 +458,16 @@
             spread_context()
         cvals = ctx[...]
         reduce_out(h, lambda zz, cvals=cvals: [dot(cvals, so[:, cols_of(y * 2 + zz)]) for y in range(4)])
-    weight_y(0)
-    weight_x(1)
+        weight_x(h)
     for h in range(2):
         total = reduce_in(h)
         xs[h] = total
         xg[h, head] = total.astype(BF16)
         ag_start(h, own_part(h))
         if h == 0:
+            weight_z(2)
             ag_forward(0)
-        else:
-            weight_z(3)
-            weight_s(0)
+            weight_y(0)
     loads[6].wait()
 
     factors = []
@@ -463,8 +478,6 @@
             acc[:, COLS:] = dot(hb, key_value_rows(shkv, zl))
             if h == 0:
                 ag_forward(1)
-                weight_y(1)
-                weight_x(2)
             ag_far(h)
             hb, more = plane(h, 1 - zl, 1)
             factor = row_factor(squares + more)
@@ -476,6 +489,21 @@
                 cz_out(c, h, i).start()
             for i in range(3):
                 cx_out(c, h, 0, i).start()
+        if h == 0:
+            weight_f(2)
+            weight_y(1)
+    weight_s(0)
+    weight_z(3)
+    weight_z(4)
+    with mark("cache_z"):
+        for h in range(2):
+            for c in range(2):
+                for m in (1, 2, 3):
+                    cz_in(c, h, m - 1).wait_recv()
+                    for i in range(3):
+                        cx_out(c, h, m, i).start()
+    weight_x(2)
+    weight_z(5)
     weight_s(1)
     weight_wait(0)
     for h in range(2):
@@ -487,16 +515,6 @@
                 full = full + dot(hb, piece_rows(0, zz))
         stack_query(h, full, factors[h])
         ag_drain(h, own_part(h))
-    with mark("cache_z"):
-        for h in range(2):
-            for c in range(2):
-                for m in (1, 2, 3):
-                    cz_in(c, h, m - 1).wait_recv()
-                    for i in range(3):
-                        cx_out(c, h, m, i).start()
-    weight_y(2)
-    weight_x(3)
-    weight_z(4)
     with mark("cache_x"):
         for h in range(2):
             for c in range(2):
@@ -504,7 +522,8 @@
                     for i in range(3):
                         cx_in(c, h, m, i).wait_recv()
                 cs_out(c, h).start()
-    weight_s(2)
+    weight_x(3)
+    weight_f(4)
     with mark("cache_s"):
         for h in range(2):
             for c in range(2):
@@ -516,6 +535,8 @@
     for section in range(3):
         for h in range(2):
             if section > 0:
+                if section == 1 and h == 0:
+                    weight_s(3)
                 if h == 0:
                     weight_wait(2 * section)
                 with mark("ag"):
@@ -564,6 +585,8 @@
                 den[...] = dens
                 oacc[...] = outs
             spread_context()
+            if section == 0 and h == 0:
+                weight_f(5)
             if h == 0:
                 weight_wait(2 * section + 1)
             cvals = ctx[...]
@@ -575,38 +598,35 @@
                 return [wide[:, y * COLS : (y + 1) * COLS] for y in range(4)]
 
             reduce_out(h, plane_of)
-            if section == 0 and h == 0:
-                weight_y(3)
-                weight_x(4)
-                weight_z(5)
-            elif section == 1 and h == 0:
-                weight_s(4)
-            elif section == 1 and h == 1:
-                weight_y(5)
+            if section == 0:
+                weight_y(2 + h)
+            elif section == 1:
+                weight_y(4 + h)
         for h in range(2):
             total = reduce_in(h)
             if section < 2:
                 xs[h] = total
                 xg[h, head] = total.astype(BF16)
                 ag_start(h, own_part(h))
+                if section == 0 and h == 0:
+                    weight_x(4)
                 if h == 0:
                     ag_forward(0)
             else:
                 out_ref[rows_half(h), :] = total
             if section == 0 and h == 0:
-                weight_s(3)
+                weight_s(2)
             elif section == 0 and h == 1:
-                weight_y(4)
                 weight_x(5)
-            elif section == 1 and h == 1:
-                weight_s(5)
+            elif section == 1:
+                weight_s(4 + h)
     for h in range(2):
         rs_drain(h)
 
     for h in range(2):
         halo_of(h).wait_send()
     for p in range(6):
-        for i in range(3):
+        for i in wz_steps(p):
             wz_out(p, i).wait_send()
         for i in range(2):
             wx_out(p, i).wait_send()
@@ -671,8 +691,8 @@
             dma((2, 8)),
             dma((2,)),
             dma((2,)),
-            dma((6, 3)),
-            dma((6, 3)),
+            dma((6, 4)),
+            dma((6, 4)),
             dma((6, 2)),
             dma((6, 2)),
             dma((6, 2)),

time: 139 us -> 122 us (0.88)
  Pallas kernels: 138 us -> 120 us
    pallas_call x1, Pallas kernels: 138 us -> 120 us  [body(): pl.pallas_call(kernel, out_shape=jax.ShapeDtypeStruct((ROWS, COLS), F32),...]
where the time goes in v3:
time: 122 us; the launch traced here: 121 us
  Pallas kernels  120 us (98%)
  local copies, waits for them, and re-layouts  1.62 us (1%)
    pallas_call x1, Pallas kernels, body(): pl.pallas_call(kernel, out_shape=jax.ShapeDtypeStruct((ROWS, COLS), F32),...  120 us

profile of v3, /device:TPU:4, one launch (start us, length us, event | category | flops | bytes accessed | tf_op | source)
XLA Modules:
  0.0 121.3 jit_solution(7195424751587197418)
XLA Ops:
  0.0 119.7 %window.1 = f32[128,384]{1,0:T(8,128)} custom-call(s32[3]{0:T(128)} %window_ref.1, s32[3,1,16]{2,1,0:T(1,128)} %blocks_ref.1, bf16[128,384]{1,0:T(8,128)(2,1)} %tokens_hbm.1, f32[5,3072]{1,0:T(8,128)} %gains_hbm.1, bf16[3072,384]{1,0:T(8,128)(2,1)} %sq_hbm.1, bf16[2,3072,128]{2,1,0:T(8,128)(2,1)} %skv_hbm.1, bf16[384,3072]{1,0:T(8,128)(2,1)} %so_hbm.1, ...), custom_call_target="tpu_custom_call" | custom-call | tf_op jit(solution)/shard_map/window/pallas_call | solution.py:660
  119.7 1.6 %copy.12 = f32[128,384]{1,0:T(8,128)} copy(f32[128,384]{1,0:T(8,128)} %window.1) | data formatting | bytes 393216

commit v4 on v3

--- a/solution.py
+++ b/solution.py
@@ -160,7 +160,7 @@
         return (cq_hbm if p % 2 == 0 else co_hbm).at[p // 2]
 
     owns = [
-        pltpu.make_async_copy(piece_source(p), wall.at[p, zh, xp, core], own_sem.at[p])
+        pltpu.make_async_copy(piece_source(p), wall.at[p, zh, xp, core], own_sem)
         for p in range(6)
     ]
     for copy in owns:
@@ -174,20 +174,22 @@
             src_ref=src, dst_ref=dst, send_sem=send, recv_sem=recv, device_id=(s, h), device_id_type=MESH
         )
 
+    def take(ref, sem):
+        pltpu.make_async_copy(ref, ref, sem).wait()
+
     beside_z = yp * 2 + 1 - zl
 
+    def ag_slot(k):
+        return 0 if k == 1 else 1 + k % 2
+
     def ag_out(h, k, src):
-        return remote(src, xg.at[h, head], ag_send.at[h, k], ag_recv.at[h, k], seq, head_to(jnp.int32(k)))
+        return remote(
+            src, xg.at[h, head], ag_send.at[h], ag_recv.at[h, ag_slot(k)], seq, head_to(jnp.int32(k))
+        )
 
     def ag_pass(h, k):
         part = xg.at[h, beside_z]
-        return remote(part, part, ag_send.at[h, k], ag_recv.at[h, k], seq, head_to(jnp.int32(k - 1)))
-
-    def ag_in(h, k):
-        return remote(
-            xg.at[h, head], xg.at[h, head_from(jnp.int32(k))], ag_send.at[h, k], ag_recv.at[h, k], seq,
-            head_to(jnp.int32(k)),
-        )
+        return remote(part, part, ag_send.at[h], ag_recv.at[h, ag_slot(k)], seq, head_to(jnp.int32(k - 1)))
 
     def ag_start(h, src):
         for k in (1, 2, 6, 4):
@@ -195,34 +197,30 @@
 
     def ag_forward(h):
         with mark("forward"):
-            ag_in(h, 1).wait_recv()
+            take(xg.at[h, 0], ag_recv.at[h, 0])
             for k in (3, 7, 5):
                 ag_pass(h, k).start()
 
     def ag_near(h):
-        for k in (2, 6, 4):
-            ag_in(h, k).wait_recv()
+        take(xg.at[h, pl.ds(0, 3)], ag_recv.at[h, 1])
 
     def ag_far(h):
-        for k in (3, 7, 5):
-            ag_in(h, k).wait_recv()
-
-    def ag_drain(h, src):
-        for k in (1, 2, 6, 4):
-            ag_out(h, k, src).wait_send()
-        for k in (3, 7, 5):
-            ag_pass(h, k).wait_send()
+        take(xg.at[h, pl.ds(0, 3)], ag_recv.at[h, 2])
+
+    def ag_drain(h):
+        take(xg.at[h, pl.ds(0, 7)], ag_send.at[h])
 
     def rs_copy(h, k):
         to = head_to(jnp.int32(k))
-        return remote(ob.at[h, to], rs.at[h, k], rs_send.at[h, k], rs_recv.at[h, k], seq, to)
+        return remote(ob.at[h, to], rs.at[h, k], rs_send.at[h], rs_recv.at[h], seq, to)
 
     beside_zh = (z_to[0], z_to[2])
     direct = (3,)
 
     def wz_copy(p, i, src, dst):
         to = beside_zh[i] if i < 2 else (z_to[1] if p in direct else beside_zh[i - 2])
-        return remote(src, dst, wz_send.at[p, i], wz_recv.at[p, i], seq_at(to, xp, core), head)
+        step = i // 2 if p not in direct else 0
+        return remote(src, dst, wz_send, wz_recv.at[p, step], seq_at(to, xp, core), head)
 
     def wz_part(p, i, zz):
         if i < 2 or p in direct:
@@ -235,38 +233,19 @@
         part = wz_part(p, i, beside_zh[3 - i])
         return wz_copy(p, i, part, part)
 
-    def wz_in(p, i):
-        part = wz_part(p, i, beside_zh[1 - i] if i < 2 else z_to[1])
-        return wz_copy(p, i, part, part)
-
-    def wz_steps(p):
-        return (0, 1, 2) if p in direct else (0, 1, 2, 3)
-
     beside = (x_to[0], x_to[2])
 
     def wx_out(p, i):
         part = wall.at[p, :, xp, core]
-        return remote(part, part, wx_send.at[p, i], wx_recv.at[p, i], seq_at(zh, beside[i], core), head)
-
-    def wx_in(p, i):
-        part = wall.at[p, :, beside[1 - i], core]
-        return remote(part, part, wx_send.at[p, i], wx_recv.at[p, i], seq_at(zh, beside[i], core), head)
+        return remote(part, part, wx_send, wx_recv.at[p], seq_at(zh, beside[i], core), head)
 
     def wy_out(p, i):
         part = wall.at[p, pl.ds(2 * i, 2), beside[1 - i], core]
-        return remote(part, part, wy_send.at[p, i], wy_recv.at[p, i], seq_at(zh, beside[i], core), head)
-
-    def wy_in(p, i):
-        part = wall.at[p, pl.ds(2 * i, 2), x_to[1], core]
-        return remote(part, part, wy_send.at[p, i], wy_recv.at[p, i], seq_at(zh, beside[i], core), head)
+        return remote(part, part, wy_send, wy_recv.at[p], seq_at(zh, beside[i], core), head)
 
     def ws_out(p):
         part = wall.at[p, :, :, core]
-        return remote(part, part, ws_send.at[p], ws_recv.at[p], sibling, head)
-
-    def ws_in(p):
-        part = wall.at[p, :, :, 1 - core]
-        return remote(part, part, ws_send.at[p], ws_recv.at[p], sibling, head)
+        return remote(part, part, ws_send, ws_recv.at[p], sibling, head)
 
     def weight_z(p):
         for i in (0, 1, 2) if p in direct else (0, 1):
@@ -274,33 +253,33 @@
 
     def weight_f(p):
         with mark("weight_f"):
+            take(wall.at[p, 0, 0], wz_recv.at[p, 0])
             for i in (0, 1):
-                wz_in(p, i).wait_recv()
                 wz_out(p, i + 2).start()
 
     def weight_x(p):
         with mark("weight_x"):
-            owns[p].wait()
-            for i in (0, 1, 2) if p in direct else (2, 3):
-                wz_in(p, i).wait_recv()
+            if p in direct:
+                take(wall.at[p, pl.ds(0, 3), 0, 0], wz_recv.at[p, 0])
+            else:
+                take(wall.at[p, 0, 0, 0], wz_recv.at[p, 1])
             for i in range(2):
                 wx_out(p, i).start()
 
     def weight_y(p):
         with mark("weight_y"):
+            take(wall.at[p, :, 0], wx_recv.at[p])
             for i in range(2):
-                wx_in(p, i).wait_recv()
                 wy_out(p, i).start()
 
     def weight_s(p):
         with mark("weight_s"):
-            for i in range(2):
-                wy_in(p, i).wait_recv()
+            take(wall.at[p, 0, pl.ds(0, 2)], wy_recv.at[p])
             ws_out(p).start()
 
     def weight_wait(p):
         with mark("weight_wait"):
-            ws_in(p).wait_recv()
+            take(wall.at[p, :, :, 0], ws_recv.at[p])
 
     cache = (kc, vc)
 
@@ -309,27 +288,19 @@
 
     def cz_out(c, h, i):
         part = cz_part(c, h, zh)
-        return remote(part, part, cz_send.at[c, h, i], cz_recv.at[c, h, i], seq_at(z_to[i], xp, core), head)
+        return remote(part, part, cz_send, cz_recv.at[c, h, i], seq_at(z_to[i], xp, core), head)
 
     def cz_in(c, h, i):
         part = cz_part(c, h, z_from[i])
-        return remote(part, part, cz_send.at[c, h, i], cz_recv.at[c, h, i], seq_at(z_to[i], xp, core), head)
+        return remote(part, part, cz_send, cz_recv.at[c, h, i], seq_at(z_to[i], xp, core), head)
 
     def cx_out(c, h, m, i):
         part = cz_part(c, h, rem(zh + 4 - m, 4))
-        return remote(part, part, cx_send.at[c, h, m, i], cx_recv.at[c, h, m, i], seq_at(zh, x_to[i], core), head)
-
-    def cx_in(c, h, m, i):
-        part = cache[c].at[rem(zh + 4 - m, 4), x_from[i], core, rows_half(h)]
-        return remote(part, part, cx_send.at[c, h, m, i], cx_recv.at[c, h, m, i], seq_at(zh, x_to[i], core), head)
+        return remote(part, part, cx_send, cx_recv.at[c, h], seq_at(zh, x_to[i], core), head)
 
     def cs_out(c, h):
         part = cache[c].at[:, :, core, rows_half(h)]
-        return remote(part, part, cs_send.at[c, h], cs_recv.at[c, h], sibling, head)
-
-    def cs_in(c, h):
-        part = cache[c].at[:, :, 1 - core, rows_half(h)]
-        return remote(part, part, cs_send.at[c, h], cs_recv.at[c, h], sibling, head)
+        return remote(part, part, cs_send, cs_recv.at[c], sibling, head)
 
     def cols_of(j):
         return pl.ds(pl.multiple_of(j * COLS, 128), COLS)
@@ -385,16 +356,14 @@
 
     def reduce_in(h):
         with mark("rs_in"):
-            for k in near + far:
-                rs_copy(h, k).wait_recv()
+            take(rs.at[h, pl.ds(1, 7)], rs_recv.at[h])
             total = xs[h] + ob[h, head].astype(F32)
             for k in near + far:
                 total = total + rs[h, k].astype(F32)
         return total
 
     def rs_drain(h):
-        for k in near + far:
-            rs_copy(h, k).wait_send()
+        take(ob.at[h, pl.ds(0, 7)], rs_send.at[h])
 
     def own_part(h):
         return xg.at[h, head]
@@ -410,7 +379,7 @@
 
     def halo_of(h):
         return remote(
-            own_kv.at[:, rows_half(h)], halo.at[:, rows_half(h)], halo_send.at[h], halo_recv.at[h], following, head
+            own_kv.at[:, rows_half(h)], halo.at[:, rows_half(h)], halo_send, halo_recv, following, head
         )
 
     for h in range(2):
@@ -433,13 +402,12 @@
             stack_query(h, full, factor)
         weight_f(h)
     for h in range(2):
-        ag_drain(h, tokens_hbm.at[rows_half(h)])
+        ag_drain(h)
 
     col = lax.broadcasted_iota(jnp.int32, (1, 2 * ROWS), 1)
     loads[5].wait()
     with mark("halo"):
-        for h in range(2):
-            halo_of(h).wait_recv()
+        take(halo, halo_recv)
     for h in range(2):
         row = lax.broadcasted_iota(jnp.int32, (HALF, 1), 0) + h * HALF
         offset = row + ROWS - col
@@ -458,6 +426,8 @@
             spread_context()
         cvals = ctx[...]
         reduce_out(h, lambda zz, cvals=cvals: [dot(cvals, so[:, cols_of(y * 2 + zz)]) for y in range(4)])
+        if h == 0:
+            take(wall.at[:, 0, 0, 0], own_sem)
         weight_x(h)
     for h in range(2):
         total = reduce_in(h)
@@ -468,6 +438,8 @@
             weight_z(2)
             ag_forward(0)
             weight_y(0)
+        else:
+            weight_z(4)
     loads[6].wait()
 
     factors = []
@@ -490,11 +462,12 @@
             for i in range(3):
                 cx_out(c, h, 0, i).start()
         if h == 0:
-            weight_f(2)
             weight_y(1)
+    weight_f(2)
+    weight_f(4)
     weight_s(0)
     weight_z(3)
-    weight_z(4)
+    weight_z(5)
     with mark("cache_z"):
         for h in range(2):
             for c in range(2):
@@ -503,7 +476,6 @@
                     for i in range(3):
                         cx_out(c, h, m, i).start()
     weight_x(2)
-    weight_z(5)
     weight_s(1)
     weight_wait(0)
     for h in range(2):
@@ -514,20 +486,15 @@
                 hb, _ = plane(h, zz, 2)
                 full = full + dot(hb, piece_rows(0, zz))
         stack_query(h, full, factors[h])
-        ag_drain(h, own_part(h))
+        ag_drain(h)
     with mark("cache_x"):
         for h in range(2):
             for c in range(2):
-                for m in range(4):
-                    for i in range(3):
-                        cx_in(c, h, m, i).wait_recv()
+                take(cache[c].at[:, pl.ds(0, 3), 0, rows_half(0)], cx_recv.at[c, h])
                 cs_out(c, h).start()
-    weight_x(3)
-    weight_f(4)
     with mark("cache_s"):
-        for h in range(2):
-            for c in range(2):
-                cs_in(c, h).wait_recv()
+        for c in range(2):
+            take(cache[c].at[:, :, 0], cs_recv.at[c])
 
     half_row = rem(lax.broadcasted_iota(jnp.int32, (GROUP * HALF, 1), 0), HALF)
     causal_col = jnp.where(col < ROWS, col, -1)
@@ -535,14 +502,18 @@
     for section in range(3):
         for h in range(2):
             if section > 0:
-                if section == 1 and h == 0:
-                    weight_s(3)
                 if h == 0:
                     weight_wait(2 * section)
                 with mark("ag"):
                     ag_near(h)
                     hb, squares = plane(h, zl, 2 + section)
                     acc[:, :COLS] = dot(hb, piece_rows(2 * section, zl))
+                    if h == 0:
+                        if section == 1:
+                            weight_x(5)
+                        ag_forward(1)
+                        if section == 1:
+                            weight_s(3)
                     ag_far(h)
                     hb, more = plane(h, 1 - zl, 2 + section)
                     full = acc[:, :COLS] + dot(hb, piece_rows(2 * section, 1 - zl))
@@ -569,9 +540,7 @@
                     best = pair if best is None else jnp.maximum(best, pair)
                 top = jnp.max(best, axis=1, keepdims=True)
             if section > 0:
-                if h == 0:
-                    ag_forward(1)
-                ag_drain(h, own_part(h))
+                ag_drain(h)
 
             with mark("value"):
                 dens, outs = None, None
@@ -585,8 +554,6 @@
                 den[...] = dens
                 oacc[...] = outs
             spread_context()
-            if section == 0 and h == 0:
-                weight_f(5)
             if h == 0:
                 weight_wait(2 * section + 1)
             cvals = ctx[...]
@@ -598,8 +565,10 @@
                 return [wide[:, y * COLS : (y + 1) * COLS] for y in range(4)]
 
             reduce_out(h, plane_of)
-            if section == 0:
-                weight_y(2 + h)
+            if section == 0 and h == 0:
+                weight_x(3)
+            elif section == 0:
+                weight_y(2)
             elif section == 1:
                 weight_y(4 + h)
         for h in range(2):
@@ -609,36 +578,29 @@
                 xg[h, head] = total.astype(BF16)
                 ag_start(h, own_part(h))
                 if section == 0 and h == 0:
+                    weight_f(5)
+                    weight_y(3)
                     weight_x(4)
                 if h == 0:
                     ag_forward(0)
             else:
                 out_ref[rows_half(h), :] = total
-            if section == 0 and h == 0:
+            if section == 0 and h == 1:
                 weight_s(2)
-            elif section == 0 and h == 1:
-                weight_x(5)
             elif section == 1:
                 weight_s(4 + h)
-    for h in range(2):
-        rs_drain(h)
-
-    for h in range(2):
-        halo_of(h).wait_send()
-    for p in range(6):
-        for i in wz_steps(p):
-            wz_out(p, i).wait_send()
-        for i in range(2):
-            wx_out(p, i).wait_send()
-            wy_out(p, i).wait_send()
-        ws_out(p).wait_send()
-    for c in range(2):
+    with mark("tail"):
         for h in range(2):
-            for i in range(3):
-                cz_out(c, h, i).wait_send()
-                for m in range(4):
-                    cx_out(c, h, m, i).wait_send()
-            cs_out(c, h).wait_send()
+            rs_drain(h)
+
+    take(own_kv, halo_send)
+    take(wall.at[pl.ds(0, 3), pl.ds(0, 3), 0], wz_send)
+    take(wall.at[:, :, 0], wx_send)
+    take(wall.at[:, pl.ds(0, 2), 0], wy_send)
+    take(wall.at[:, :, :, 0], ws_send)
+    take(kc.at[pl.ds(0, 3), 0], cz_send)
+    take(kc.at[pl.ds(0, 3)], cx_send)
+    take(kc, cs_send)
 
 
 def body(
@@ -684,27 +646,27 @@
             pltpu.VMEM((GROUP * HALF, HEAD), F32),
             pltpu.VMEM((GROUP * HALF, HEAD), F32),
             dma((7,)),
-            dma((6,)),
-            dma((2, 8)),
-            dma((2, 8)),
-            dma((2, 8)),
-            dma((2, 8)),
+            dma,
+            dma((2,)),
+            dma((2, 3)),
             dma((2,)),
             dma((2,)),
-            dma((6, 4)),
-            dma((6, 4)),
+            dma,
+            dma,
+            dma,
             dma((6, 2)),
-            dma((6, 2)),
-            dma((6, 2)),
-            dma((6, 2)),
+            dma,
             dma((6,)),
+            dma,
             dma((6,)),
+            dma,
+            dma((6,)),
+            dma,
             dma((2, 2, 3)),
-            dma((2, 2, 3)),
-            dma((2, 2, 4, 3)),
-            dma((2, 2, 4, 3)),
+            dma,
             dma((2, 2)),
-            dma((2, 2)),
+            dma,
+            dma((2,)),
         ],
         compiler_params=pltpu.CompilerParams(
             collective_id=0, has_side_effects=True, vmem_limit_bytes=60 * 1024 * 1024

time: 122 us -> 119 us (0.975)
  Pallas kernels: 120 us -> 116 us
    pallas_call x1, Pallas kernels: 120 us -> 116 us  [body(): pl.pallas_call(kernel, out_shape=jax.ShapeDtypeStruct((ROWS, COLS), F32),...]
where the time goes in v4:
time: 119 us; the launch traced here: 117 us
  Pallas kernels  116 us (97%)
  local copies, waits for them, and re-layouts  1.62 us (1%)
    pallas_call x1, Pallas kernels, body(): pl.pallas_call(kernel, out_shape=jax.ShapeDtypeStruct((ROWS, COLS), F32),...  116 us

profile of v4, /device:TPU:4, one launch (start us, length us, event | category | flops | bytes accessed | tf_op | source)
XLA Modules:
  0.0 117.4 jit_solution(2498618893298663907)
XLA Ops:
  0.0 115.8 %window.1 = f32[128,384]{1,0:T(8,128)} custom-call(s32[3]{0:T(128)} %window_ref.1, s32[3,1,16]{2,1,0:T(1,128)} %blocks_ref.1, bf16[128,384]{1,0:T(8,128)(2,1)} %tokens_hbm.1, f32[5,3072]{1,0:T(8,128)} %gains_hbm.1, bf16[3072,384]{1,0:T(8,128)(2,1)} %sq_hbm.1, bf16[2,3072,128]{2,1,0:T(8,128)(2,1)} %skv_hbm.1, bf16[384,3072]{1,0:T(8,128)(2,1)} %so_hbm.1, ...), custom_call_target="tpu_custom_call" | custom-call | tf_op jit(solution)/shard_map/window/pallas_call | solution.py:622
  115.8 1.6 %copy.12 = f32[128,384]{1,0:T(8,128)} copy(f32[128,384]{1,0:T(8,128)} %window.1) | data formatting | bytes 393216

commit v5 on v4

--- a/solution.py
+++ b/solution.py
@@ -84,8 +84,10 @@
     wz_send,
     wz_recv,
     wx_send,
+    wx_first,
     wx_recv,
     wy_send,
+    wy_first,
     wy_recv,
     ws_send,
     ws_recv,
@@ -235,13 +237,27 @@
 
     beside = (x_to[0], x_to[2])
 
-    def wx_out(p, i):
-        part = wall.at[p, :, xp, core]
-        return remote(part, part, wx_send, wx_recv.at[p], seq_at(zh, beside[i], core), head)
-
-    def wy_out(p, i):
-        part = wall.at[p, pl.ds(2 * i, 2), beside[1 - i], core]
-        return remote(part, part, wy_send, wy_recv.at[p], seq_at(zh, beside[i], core), head)
+    others = [rem(zh + d, 4) for d in (1, 2, 3)]
+
+    def wx_out(p, zz, i, recv):
+        src = piece_source(p) if zz is zh else wall.at[p, zz, xp, core]
+        return remote(src, wall.at[p, zz, xp, core], wx_send, recv, seq_at(zh, beside[i], core), head)
+
+    def wy_out(p, zz, i, recv):
+        part = wall.at[p, zz, beside[1 - i], core, pl.ds(i * (PIECE // 2), PIECE // 2)]
+        return remote(part, part, wy_send, recv, seq_at(zh, beside[i], core), head)
+
+    def own_row_x():
+        for p in range(6):
+            for i in range(2):
+                wx_out(p, zh, i, wx_first).start()
+
+    def own_row_y():
+        with mark("own_row_y"):
+            take(wall.at[:, 0, 0], wx_first)
+            for p in range(6):
+                for i in range(2):
+                    wy_out(p, zh, i, wy_first).start()
 
     def ws_out(p):
         part = wall.at[p, :, :, core]
@@ -263,18 +279,22 @@
                 take(wall.at[p, pl.ds(0, 3), 0, 0], wz_recv.at[p, 0])
             else:
                 take(wall.at[p, 0, 0, 0], wz_recv.at[p, 1])
-            for i in range(2):
-                wx_out(p, i).start()
+            for zz in others:
+                for i in range(2):
+                    wx_out(p, zz, i, wx_recv.at[p]).start()
 
     def weight_y(p):
         with mark("weight_y"):
-            take(wall.at[p, :, 0], wx_recv.at[p])
-            for i in range(2):
-                wy_out(p, i).start()
+            take(wall.at[p, pl.ds(0, 3), 0], wx_recv.at[p])
+            for zz in others:
+                for i in range(2):
+                    wy_out(p, zz, i, wy_recv.at[p]).start()
 
     def weight_s(p):
         with mark("weight_s"):
-            take(wall.at[p, 0, pl.ds(0, 2)], wy_recv.at[p])
+            if p == 0:
+                take(wall.at[:, 0, 0, 0], wy_first)
+            take(wall.at[p, pl.ds(0, 3), 0, 0], wy_recv.at[p])
             ws_out(p).start()
 
     def weight_wait(p):
@@ -371,6 +391,7 @@
     for h in range(2):
         ag_start(h, tokens_hbm.at[rows_half(h)])
     weight_z(0)
+    own_row_x()
     for h in range(2):
         ag_forward(h)
     weight_z(1)
@@ -401,6 +422,7 @@
             )
             stack_query(h, full, factor)
         weight_f(h)
+    own_row_y()
     for h in range(2):
         ag_drain(h)
 
@@ -512,8 +534,7 @@
                         if section == 1:
                             weight_x(5)
                         ag_forward(1)
-                        if section == 1:
-                            weight_s(3)
+                        weight_s(3 if section == 1 else 5)
                     ag_far(h)
                     hb, more = plane(h, 1 - zl, 2 + section)
                     full = acc[:, :COLS] + dot(hb, piece_rows(2 * section, 1 - zl))
@@ -581,14 +602,13 @@
                     weight_f(5)
                     weight_y(3)
                     weight_x(4)
+                    weight_s(2)
+                elif section == 1 and h == 0:
+                    weight_s(4)
                 if h == 0:
                     ag_forward(0)
             else:
                 out_ref[rows_half(h), :] = total
-            if section == 0 and h == 1:
-                weight_s(2)
-            elif section == 1:
-                weight_s(4 + h)
     with mark("tail"):
         for h in range(2):
             rs_drain(h)
@@ -656,7 +676,9 @@
             dma,
             dma((6, 2)),
             dma,
+            dma,
             dma((6,)),
+            dma,
             dma,
             dma((6,)),
             dma,

time: 119 us -> 117 us (0.983); the launches traced: 117 us -> 117 us
  no operation moved by 1% of the time
where the time goes in v5:
time: 117 us
  Pallas kernels  115 us (98%)
  local copies, waits for them, and re-layouts  1.62 us (1%)
    pallas_call x1, Pallas kernels, body(): pl.pallas_call(kernel, out_shape=jax.ShapeDtypeStruct((ROWS, COLS), F32),...  115 us

profile of v5, /device:TPU:4, one launch (start us, length us, event | category | flops | bytes accessed | tf_op | source)
XLA Modules:
  0.0 116.7 jit_solution(6899244321400224418)
XLA Ops:
  0.0 115.1 %window.1 = f32[128,384]{1,0:T(8,128)} custom-call(s32[3]{0:T(128)} %window_ref.1, s32[3,1,16]{2,1,0:T(1,128)} %blocks_ref.1, bf16[128,384]{1,0:T(8,128)(2,1)} %tokens_hbm.1, f32[5,3072]{1,0:T(8,128)} %gains_hbm.1, bf16[3072,384]{1,0:T(8,128)(2,1)} %sq_hbm.1, bf16[2,3072,128]{2,1,0:T(8,128)(2,1)} %skv_hbm.1, bf16[384,3072]{1,0:T(8,128)(2,1)} %so_hbm.1, ...), custom_call_target="tpu_custom_call" | custom-call | tf_op jit(solution)/shard_map/window/pallas_call | solution.py:642
  115.1 1.6 %copy.12 = f32[128,384]{1,0:T(8,128)} copy(f32[128,384]{1,0:T(8,128)} %window.1) | data formatting | bytes 393216

commit v6 on v5

--- a/solution.py
+++ b/solution.py
@@ -515,8 +515,7 @@
                 take(cache[c].at[:, pl.ds(0, 3), 0, rows_half(0)], cx_recv.at[c, h])
                 cs_out(c, h).start()
     with mark("cache_s"):
-        for c in range(2):
-            take(cache[c].at[:, :, 0], cs_recv.at[c])
+        take(kc.at[:, :, 0], cs_recv.at[0])
 
     half_row = rem(lax.broadcasted_iota(jnp.int32, (GROUP * HALF, 1), 0), HALF)
     causal_col = jnp.where(col < ROWS, col, -1)
@@ -563,6 +562,9 @@
             if section > 0:
                 ag_drain(h)
 
+            if section == 0 and h == 0:
+                with mark("cache_v"):
+                    take(vc.at[:, :, 0], cs_recv.at[1])
             with mark("value"):
                 dens, outs = None, None
                 for i in range(8):

time: 117 us -> 120 us (1.026)
  Pallas kernels: 115 us -> 118 us
    pallas_call x1, Pallas kernels: 115 us -> 118 us  [body(): pl.pallas_call(kernel, out_shape=jax.ShapeDtypeStruct((ROWS, COLS), F32),...]
where the time goes in v6:
time: 120 us; the launch traced here: 119 us
  Pallas kernels  118 us (98%)
  local copies, waits for them, and re-layouts  1.62 us (1%)
    pallas_call x1, Pallas kernels, body(): pl.pallas_call(kernel, out_shape=jax.ShapeDtypeStruct((ROWS, COLS), F32),...  118 us

profile of v6, /device:TPU:4, one launch (start us, length us, event | category | flops | bytes accessed | tf_op | source)
XLA Modules:
  0.0 119.4 jit_solution(17349529530625033866)
XLA Ops:
  0.0 117.8 %window.1 = f32[128,384]{1,0:T(8,128)} custom-call(s32[3]{0:T(128)} %window_ref.1, s32[3,1,16]{2,1,0:T(1,128)} %blocks_ref.1, bf16[128,384]{1,0:T(8,128)(2,1)} %tokens_hbm.1, f32[5,3072]{1,0:T(8,128)} %gains_hbm.1, bf16[3072,384]{1,0:T(8,128)(2,1)} %sq_hbm.1, bf16[2,3072,128]{2,1,0:T(8,128)(2,1)} %skv_hbm.1, bf16[384,3072]{1,0:T(8,128)(2,1)} %so_hbm.1, ...), custom_call_target="tpu_custom_call" | custom-call | tf_op jit(solution)/shard_map/window/pallas_call | solution.py:644
  117.8 1.6 %copy.12 = f32[128,384]{1,0:T(8,128)} copy(f32[128,384]{1,0:T(8,128)} %window.1) | data formatting | bytes 393216
